TPU v7x, 512 devices: a whole 4x4x16 slice. The times are simulated.
512 devices in a mesh: flow: 8 (over y, core), cross: 64 (over x, z).
Axes of the slice: x: 4, y: 4, z: 16, core: 2. Of those that a mesh axis runs over, the one named last changes fastest.
Arguments:
- source: float32 [16, 64, 131072], P('flow', None, 'cross'), may hold values from -6 to 6
- cotangent: float32 [16, 64, 131072], P('flow', None, 'cross'), may hold values from -6 to 6
- flux: float32 [16, 131072], P('flow', 'cross'), may hold values from 0.3 to 1
- pore_mask: int32 [16, 131072], P('flow', 'cross'), may hold values 0 or 1
- upwind: int32 [16, 131072], P('flow', 'cross'), may hold values 0 or 1
- side_link: int32 [16, 131072], P('flow', 'cross'), may hold values from 0 to 159
- local_inverse: float32 [64, 64], replicated, may hold values from -0.75 to 0.75
- flow_lift: float32 [64, 16], replicated, may hold values from -2 to 2
- side_lift: float32 [64, 16], replicated, may hold values from -2 to 2
- flow_trace: float32 [16, 64], replicated, may hold values from -0.75 to 0.75
- side_trace: float32 [16, 64], replicated, may hold values from -0.75 to 0.75
Outputs:
- concentration: float32 [16, 64, 131072], P('flow', None, 'cross')
- sensitivity: float32 [16, 64, 131072], P('flow', None, 'cross')
Inputs may be any that keep to these rules, and one draw needn't show every extreme that they name: `side_link`: entries 0 to 15 name the left cross neighbour's edge elements, 16 to 143 the tile's own slots, the rest the right neighbour's edge elements.
All inputs are finite; a program needn't handle non-finite values. No bound on the sum of `pore_mask` or of `upwind` on one device may be relied on, other than what follows from the above.
Results may differ from a plain program's by a relative error of at most 0.00012.
Values sent between devices are 32-bit elements; how exact they have to be, the bound alone decides.
A program may use at most 64 MiB of HBM per device.

v0:
```python
import jax
import jax.numpy as jnp
from jax import lax
from jax.sharding import PartitionSpec as P

FACE = 16
TILE = 128
HALO = 16


HIGH = lax.Precision.HIGHEST


def with_halo(cells, sides, width):
    for axis, dim in sides:
        count = lax.axis_size(axis)
        ends = count - 1
        head = lax.slice_in_dim(cells, 0, width, axis=dim)
        tail = lax.slice_in_dim(cells, cells.shape[dim] - width, cells.shape[dim], axis=dim)
        cells = jnp.concatenate(
            [
                lax.ppermute(tail, axis, [(i, (i + 1) % count) for i in range(ends)]),
                cells,
                lax.ppermute(head, axis, [((i + 1) % count, i) for i in range(ends)]),
            ],
            axis=dim,
        )
    return cells


def passed_along(value, axis, steps):
    count = lax.axis_size(axis)
    leading, last = (max(0, -steps), min(count, count - steps))
    return lax.ppermute(value, axis, [(source, source + steps) for source in range(leading, last)])


def matmul(left, right):
    return jnp.dot(left, right, precision=HIGH)


def sweep_forward(
    inbound, base, flux, pore_mask, upwind, side_link, flow_lift, side_lift, flow_trace, side_trace
):
    tiles_here = base.shape[2] // TILE
    columns = lax.broadcasted_iota(jnp.int32, (1, 1, TILE + 2 * HALO), 2)

    def level(carry, inputs):
        flow_in = carry[0]
        side_rows = carry[1]
        based, coeff, live, inflow, links = inputs
        extended = with_halo(side_rows.reshape(FACE, tiles_here, TILE), (("cross", 2),), HALO)
        picker = (links.reshape(tiles_here, TILE, 1) == columns).astype(
            jnp.float32
        ) * inflow.reshape(tiles_here, TILE, 1).astype(jnp.float32)
        side_in = jnp.einsum("fck,cjk->fcj", extended, picker, precision=HIGH).reshape(FACE, -1)
        lifted = matmul(flow_lift, flow_in) + matmul(side_lift, side_in)
        conc = live.astype(jnp.float32) * (based + coeff * lifted)
        return (jnp.stack([matmul(flow_trace, conc), matmul(side_trace, conc)]), conc)

    final, concs = lax.scan(level, inbound, (base, flux, pore_mask, upwind, side_link))
    return (concs, final)


def sweep_adjoint(
    inbound,
    cotangent,
    flux,
    pore_mask,
    upwind,
    side_link,
    local_inverse,
    flow_lift,
    side_lift,
    flow_trace,
    side_trace,
):
    tiles_here = cotangent.shape[2] // TILE
    columns = lax.broadcasted_iota(jnp.int32, (1, 1, TILE + 2 * HALO), 2)

    def level(carry, inputs):
        back_flow = carry[0]
        back_side = carry[1]
        weights, coeff, live, inflow, links = inputs
        gathered = weights + matmul(flow_trace.T, back_flow) + matmul(side_trace.T, back_side)
        masked = live.astype(jnp.float32) * gathered
        sens = matmul(local_inverse.T, masked)
        prev_flow = coeff * matmul(flow_lift.T, masked)
        prev_side = inflow.astype(jnp.float32) * coeff * matmul(side_lift.T, masked)
        picker = (links.reshape(tiles_here, TILE, 1) == columns).astype(jnp.float32)
        spread = jnp.einsum(
            "fcj,cjk->fck", prev_side.reshape(FACE, tiles_here, TILE), picker, precision=HIGH
        )
        own = spread[:, :, HALO : HALO + TILE]
        edges = jnp.concatenate([spread[:, :, :HALO], spread[:, :, HALO + TILE :]], axis=2)
        returned = with_halo(edges, (("cross", 2),), HALO)
        own = own.at[:, :, :HALO].add(returned[:, :, :HALO])
        own = own.at[:, :, TILE - HALO :].add(returned[:, :, 3 * HALO :])
        return (jnp.stack([prev_flow, own.reshape(FACE, -1)]), sens)

    final, sens_all = lax.scan(
        level, inbound, (cotangent, flux, pore_mask, upwind, side_link), reverse=True
    )
    return (sens_all, final)


def per_device(
    source,
    cotangent,
    flux,
    pore_mask,
    upwind,
    side_link,
    local_inverse,
    flow_lift,
    side_lift,
    flow_trace,
    side_trace,
):
    base = jnp.einsum("mn,lne->lme", local_inverse, source, precision=HIGH)
    elems = source.shape[2]
    pieces = 1
    width = elems // pieces
    lanes = lax.axis_size("flow")
    place = lax.axis_index("flow")
    rounds = lanes + pieces - 1

    def cut_all(arrays):
        return [item for item in arrays]

    def forward_round(step, conc_out, inbound):
        slot = step - place
        valid = (slot >= 0) & (slot < pieces)
        based, coeff, live, inflow, links = cut_all([base, flux, pore_mask, upwind, side_link])
        concs, final = sweep_forward(
            inbound, based, coeff, live, inflow, links, flow_lift, side_lift, flow_trace, side_trace
        )
        conc_out = jnp.where(valid, concs, conc_out)
        inbound = passed_along(final, "flow", 1)
        return (conc_out, inbound)

    def adjoint_round(step, sens_out, inbound):
        slot = step - (lanes - 1 - place)
        valid = (slot >= 0) & (slot < pieces)
        weights, coeff, live, inflow, links = cut_all(
            [cotangent, flux, pore_mask, upwind, side_link]
        )
        sens_all, final = sweep_adjoint(
            inbound,
            weights,
            coeff,
            live,
            inflow,
            links,
            local_inverse,
            flow_lift,
            side_lift,
            flow_trace,
            side_trace,
        )
        sens_out = jnp.where(valid, sens_all, sens_out)
        inbound = passed_along(final, "flow", -1)
        return (sens_out, inbound)

    empty_field = jnp.zeros(source.shape, jnp.float32)
    empty_trace = jnp.zeros((2, FACE, width), jnp.float32)

    def forward_only(step, state):
        return forward_round(step, state[0], state[1])

    def adjoint_only(step, state):
        return adjoint_round(step, state[0], state[1])

    conc_out, fwd_in = lax.fori_loop(0, rounds, forward_only, (empty_field, empty_trace))
    sens_out, adj_in = lax.fori_loop(0, rounds, adjoint_only, (empty_field, empty_trace))
    return (conc_out, sens_out)


def solution(mesh):
    placed = (
        P("flow", None, "cross"),
        P("flow", None, "cross"),
        P("flow", "cross"),
        P("flow", "cross"),
        P("flow", "cross"),
        P("flow", "cross"),
        P(),
        P(),
        P(),
        P(),
        P(),
    )
    return jax.shard_map(
        per_device,
        mesh=mesh,
        in_specs=placed,
        out_specs=(P("flow", None, "cross"), P("flow", None, "cross")),
        check_vma=False,
    )
```

profile of v0, /device:TPU:15, one launch (start us, length us, event | category | flops | bytes accessed | tf_op | source)
XLA Modules:
  0.0 700.9 jit_solution(7592753404639508167)
XLA Ops:
  3.8 360.4 %while.121 = (s32[]{:T(128)}, f32[2,64,2048]{2,1,0:T(8,128)}, f32[2,16,2048]{2,1,0:T(8,128)S(1)}, s32[]{:T(128)}, s32[2,2048]{1,0:T(2,128)}, /*index=5*/f32[2,64...) while((s32[]{:T(128)}, f32[2,64,2048]{2,1,0:T(8,128)}, ...), condition=%wide.region_3.4_spmd.clone, body=%wide.region_0.3_spmd.clone.sunk | while | flops 165433344 | bytes 20353784 | solution.py:173
  4.9 41.7 %while.124 = (s32[]{:T(128)}, f32[2,16,2048]{2,1,0:T(8,128)S(1)}, f32[2,64,2048]{2,1,0:T(8,128)}, s32[2,2048]{1,0:T(2,128)}, f32[2,64,2048]{2,1,0:T(8,128)S(1)},...) while((s32[]{:T(128)}, f32[2,16,2048]{2,1,0:T(8,128)S(1)}, ...), condition=%wide.region_2.2_spmd.clone, body=%wide.region_1.1_spmd.clone.sunk | while | flops 164909056 | bytes 14586253 | solution.py:60
  5.7 11.4 %collective-permute-start.3 = (f32[16,16,16]{2,0,1:T(8,128)}, f32[16,16,16]{2,0,1:T(8,128)}, u32[]{:S(2)}, u32[]{:S(2)}) collective-permute-start(f32[16,16,16]{2,0,1:T(8,128)} %get-tuple-element.1724), channel_id=1, source_target_pairs={{1,0},{2,1},{3,2},{4,3},{5,4},{6,5},{7,6},{8,7},{9,8},{10,9},{11,1... | collective-permute-start | bytes 49160 | tf_op jit(solution)/shard_map/while/body/eval_jaxpr/while/body/eval_jaxpr/ppermute | solution.py:24
  57.6 32.2 %while.124 = (s32[]{:T(128)}, f32[2,16,2048]{2,1,0:T(8,128)S(1)}, f32[2,64,2048]{2,1,0:T(8,128)}, s32[2,2048]{1,0:T(2,128)}, f32[2,64,2048]{2,1,0:T(8,128)S(1)},...) while((s32[]{:T(128)}, f32[2,16,2048]{2,1,0:T(8,128)S(1)}, ...), condition=%wide.region_2.2_spmd.clone, body=%wide.region_1.1_spmd.clone.sunk | while | flops 164909056 | bytes 14586253 | solution.py:60
  89.9 6.4 collective-permute-start.5
  101.6 32.2 %while.124 = (s32[]{:T(128)}, f32[2,16,2048]{2,1,0:T(8,128)S(1)}, f32[2,64,2048]{2,1,0:T(8,128)}, s32[2,2048]{1,0:T(2,128)}, f32[2,64,2048]{2,1,0:T(8,128)S(1)},...) while((s32[]{:T(128)}, f32[2,16,2048]{2,1,0:T(8,128)S(1)}, ...), condition=%wide.region_2.2_spmd.clone, body=%wide.region_1.1_spmd.clone.sunk | while | flops 164909056 | bytes 14586253 | solution.py:60
  133.8 6.4 collective-permute-start.5
  145.5 32.2 %while.124 = (s32[]{:T(128)}, f32[2,16,2048]{2,1,0:T(8,128)S(1)}, f32[2,64,2048]{2,1,0:T(8,128)}, s32[2,2048]{1,0:T(2,128)}, f32[2,64,2048]{2,1,0:T(8,128)S(1)},...) while((s32[]{:T(128)}, f32[2,16,2048]{2,1,0:T(8,128)S(1)}, ...), condition=%wide.region_2.2_spmd.clone, body=%wide.region_1.1_spmd.clone.sunk | while | flops 164909056 | bytes 14586253 | solution.py:60
  177.8 6.4 collective-permute-start.5
  189.5 32.2 %while.124 = (s32[]{:T(128)}, f32[2,16,2048]{2,1,0:T(8,128)S(1)}, f32[2,64,2048]{2,1,0:T(8,128)}, s32[2,2048]{1,0:T(2,128)}, f32[2,64,2048]{2,1,0:T(8,128)S(1)},...) while((s32[]{:T(128)}, f32[2,16,2048]{2,1,0:T(8,128)S(1)}, ...), condition=%wide.region_2.2_spmd.clone, body=%wide.region_1.1_spmd.clone.sunk | while | flops 164909056 | bytes 14586253 | solution.py:60
  221.7 6.4 collective-permute-start.5
  233.4 32.2 %while.124 = (s32[]{:T(128)}, f32[2,16,2048]{2,1,0:T(8,128)S(1)}, f32[2,64,2048]{2,1,0:T(8,128)}, s32[2,2048]{1,0:T(2,128)}, f32[2,64,2048]{2,1,0:T(8,128)S(1)},...) while((s32[]{:T(128)}, f32[2,16,2048]{2,1,0:T(8,128)S(1)}, ...), condition=%wide.region_2.2_spmd.clone, body=%wide.region_1.1_spmd.clone.sunk | while | flops 164909056 | bytes 14586253 | solution.py:60
  265.6 6.4 collective-permute-start.5
  277.4 32.2 %while.124 = (s32[]{:T(128)}, f32[2,16,2048]{2,1,0:T(8,128)S(1)}, f32[2,64,2048]{2,1,0:T(8,128)}, s32[2,2048]{1,0:T(2,128)}, f32[2,64,2048]{2,1,0:T(8,128)S(1)},...) while((s32[]{:T(128)}, f32[2,16,2048]{2,1,0:T(8,128)S(1)}, ...), condition=%wide.region_2.2_spmd.clone, body=%wide.region_1.1_spmd.clone.sunk | while | flops 164909056 | bytes 14586253 | solution.py:60
  309.6 6.4 collective-permute-start.5
  321.3 32.2 %while.124 = (s32[]{:T(128)}, f32[2,16,2048]{2,1,0:T(8,128)S(1)}, f32[2,64,2048]{2,1,0:T(8,128)}, s32[2,2048]{1,0:T(2,128)}, f32[2,64,2048]{2,1,0:T(8,128)S(1)},...) while((s32[]{:T(128)}, f32[2,16,2048]{2,1,0:T(8,128)S(1)}, ...), condition=%wide.region_2.2_spmd.clone, body=%wide.region_1.1_spmd.clone.sunk | while | flops 164909056 | bytes 14586253 | solution.py:60
  353.5 6.4 collective-permute-start.5
  364.2 336.7 %while.123 = (s32[]{:T(128)}, f32[2,64,2048]{2,1,0:T(8,128)}, f32[2,16,2048]{2,1,0:T(8,128)S(1)}, s32[]{:T(128)}, f32[2,2048]{1,0:T(2,128)}, /*index=5*/s32[2,20...) while((s32[]{:T(128)}, f32[2,64,2048]{2,1,0:T(8,128)}, ...), condition=%wide.region_7.8_spmd.clone, body=%wide.region_4.7_spmd.clone.sunk | while | flops 265631744 | bytes 12968838 | solution.py:174
  365.5 31.1 %while.125 = (s32[]{:T(128)}, f32[2,16,2048]{2,1,0:T(8,128)S(1)}, f32[2,64,2048]{2,1,0:T(8,128)}, f32[2,2048]{1,0:T(2,128)S(1)}, s32[2,2048]{1,0:T(2,128)S(1)}, ...) while((s32[]{:T(128)}, f32[2,16,2048]{2,1,0:T(8,128)S(1)}, ...), condition=%wide.region_6.6_spmd.clone, body=%wide.region_5.5_spmd.clone.sunk | while | flops 265107456 | bytes 6824201 | solution.py:100
  408.1 32.8 %while.125 = (s32[]{:T(128)}, f32[2,16,2048]{2,1,0:T(8,128)S(1)}, f32[2,64,2048]{2,1,0:T(8,128)}, f32[2,2048]{1,0:T(2,128)S(1)}, s32[2,2048]{1,0:T(2,128)S(1)}, ...) while((s32[]{:T(128)}, f32[2,16,2048]{2,1,0:T(8,128)S(1)}, ...), condition=%wide.region_6.6_spmd.clone, body=%wide.region_5.5_spmd.clone.sunk | while | flops 265107456 | bytes 6824201 | solution.py:100
  450.0 32.9 %while.125 = (s32[]{:T(128)}, f32[2,16,2048]{2,1,0:T(8,128)S(1)}, f32[2,64,2048]{2,1,0:T(8,128)}, f32[2,2048]{1,0:T(2,128)S(1)}, s32[2,2048]{1,0:T(2,128)S(1)}, ...) while((s32[]{:T(128)}, f32[2,16,2048]{2,1,0:T(8,128)S(1)}, ...), condition=%wide.region_6.6_spmd.clone, body=%wide.region_5.5_spmd.clone.sunk | while | flops 265107456 | bytes 6824201 | solution.py:100
  454.9 6.2 collective-permute-start.1
  492.0 32.9 %while.125 = (s32[]{:T(128)}, f32[2,16,2048]{2,1,0:T(8,128)S(1)}, f32[2,64,2048]{2,1,0:T(8,128)}, f32[2,2048]{1,0:T(2,128)S(1)}, s32[2,2048]{1,0:T(2,128)S(1)}, ...) while((s32[]{:T(128)}, f32[2,16,2048]{2,1,0:T(8,128)S(1)}, ...), condition=%wide.region_6.6_spmd.clone, body=%wide.region_5.5_spmd.clone.sunk | while | flops 265107456 | bytes 6824201 | solution.py:100
  496.9 6.2 collective-permute-start.1
  534.0 32.9 %while.125 = (s32[]{:T(128)}, f32[2,16,2048]{2,1,0:T(8,128)S(1)}, f32[2,64,2048]{2,1,0:T(8,128)}, f32[2,2048]{1,0:T(2,128)S(1)}, s32[2,2048]{1,0:T(2,128)S(1)}, ...) while((s32[]{:T(128)}, f32[2,16,2048]{2,1,0:T(8,128)S(1)}, ...), condition=%wide.region_6.6_spmd.clone, body=%wide.region_5.5_spmd.clone.sunk | while | flops 265107456 | bytes 6824201 | solution.py:100
  538.9 6.2 collective-permute-start.1
  576.0 32.9 %while.125 = (s32[]{:T(128)}, f32[2,16,2048]{2,1,0:T(8,128)S(1)}, f32[2,64,2048]{2,1,0:T(8,128)}, f32[2,2048]{1,0:T(2,128)S(1)}, s32[2,2048]{1,0:T(2,128)S(1)}, ...) while((s32[]{:T(128)}, f32[2,16,2048]{2,1,0:T(8,128)S(1)}, ...), condition=%wide.region_6.6_spmd.clone, body=%wide.region_5.5_spmd.clone.sunk | while | flops 265107456 | bytes 6824201 | solution.py:100
  580.9 6.2 collective-permute-start.1
  618.0 32.9 %while.125 = (s32[]{:T(128)}, f32[2,16,2048]{2,1,0:T(8,128)S(1)}, f32[2,64,2048]{2,1,0:T(8,128)}, f32[2,2048]{1,0:T(2,128)S(1)}, s32[2,2048]{1,0:T(2,128)S(1)}, ...) while((s32[]{:T(128)}, f32[2,16,2048]{2,1,0:T(8,128)S(1)}, ...), condition=%wide.region_6.6_spmd.clone, body=%wide.region_5.5_spmd.clone.sunk | while | flops 265107456 | bytes 6824201 | solution.py:100
  623.0 6.2 collective-permute-start.1
  660.1 32.9 %while.125 = (s32[]{:T(128)}, f32[2,16,2048]{2,1,0:T(8,128)S(1)}, f32[2,64,2048]{2,1,0:T(8,128)}, f32[2,2048]{1,0:T(2,128)S(1)}, s32[2,2048]{1,0:T(2,128)S(1)}, ...) while((s32[]{:T(128)}, f32[2,16,2048]{2,1,0:T(8,128)S(1)}, ...), condition=%wide.region_6.6_spmd.clone, body=%wide.region_5.5_spmd.clone.sunk | while | flops 265107456 | bytes 6824201 | solution.py:100
  665.0 6.2 collective-permute-start.1
  (1005 shorter events, 600.7 us)
Async XLA Ops:
  5.7 16.7 %collective-permute-start.3 = (f32[16,16,16]{2,0,1:T(8,128)}, f32[16,16,16]{2,0,1:T(8,128)}, u32[]{:S(2)}, u32[]{:S(2)}) collective-permute-start(f32[16,16,16]{2,0,1:T(8,128)} %get-tuple-element.1724), channel_id=1, source_target_pairs={{1,0},{2,1},{3,2},{4,3},{5,4},{6,5},{7,6},{8,7},{9,8},{10,9},{11,1... | collective-permute-start | bytes 49160 | tf_op jit(solution)/shard_map/while/body/eval_jaxpr/while/body/eval_jaxpr/ppermute | solution.py:24
  46.6 9.1 %collective-permute-start.5 = (f32[2,16,2048]{2,1,0:T(8,128)S(1)}, f32[2,16,2048]{2,1,0:T(8,128)}, u32[]{:S(2)}, u32[]{:S(2)}) collective-permute-start(f32[2,16,2048]{2,1,0:T(8,128)S(1)} %get-tuple-element.1672), channel_id=1, source_target_pairs={{0,64},{64,128},{128,192},{192,256},{256,320},{320,384},{384,448},... | collective-permute-start | bytes 786440 | tf_op jit(solution)/shard_map/while/body/eval_jaxpr/ppermute | solution.py:34
  89.9 9.7 %collective-permute-start.5 = (f32[2,16,2048]{2,1,0:T(8,128)S(1)}, f32[2,16,2048]{2,1,0:T(8,128)}, u32[]{:S(2)}, u32[]{:S(2)}) collective-permute-start(f32[2,16,2048]{2,1,0:T(8,128)S(1)} %get-tuple-element.1672), channel_id=1, source_target_pairs={{0,64},{64,128},{128,192},{192,256},{256,320},{320,384},{384,448},... | collective-permute-start | bytes 786440 | tf_op jit(solution)/shard_map/while/body/eval_jaxpr/ppermute | solution.py:34
  133.8 9.7 %collective-permute-start.5 = (f32[2,16,2048]{2,1,0:T(8,128)S(1)}, f32[2,16,2048]{2,1,0:T(8,128)}, u32[]{:S(2)}, u32[]{:S(2)}) collective-permute-start(f32[2,16,2048]{2,1,0:T(8,128)S(1)} %get-tuple-element.1672), channel_id=1, source_target_pairs={{0,64},{64,128},{128,192},{192,256},{256,320},{320,384},{384,448},... | collective-permute-start | bytes 786440 | tf_op jit(solution)/shard_map/while/body/eval_jaxpr/ppermute | solution.py:34
  177.8 9.7 %collective-permute-start.5 = (f32[2,16,2048]{2,1,0:T(8,128)S(1)}, f32[2,16,2048]{2,1,0:T(8,128)}, u32[]{:S(2)}, u32[]{:S(2)}) collective-permute-start(f32[2,16,2048]{2,1,0:T(8,128)S(1)} %get-tuple-element.1672), channel_id=1, source_target_pairs={{0,64},{64,128},{128,192},{192,256},{256,320},{320,384},{384,448},... | collective-permute-start | bytes 786440 | tf_op jit(solution)/shard_map/while/body/eval_jaxpr/ppermute | solution.py:34
  221.7 9.7 %collective-permute-start.5 = (f32[2,16,2048]{2,1,0:T(8,128)S(1)}, f32[2,16,2048]{2,1,0:T(8,128)}, u32[]{:S(2)}, u32[]{:S(2)}) collective-permute-start(f32[2,16,2048]{2,1,0:T(8,128)S(1)} %get-tuple-element.1672), channel_id=1, source_target_pairs={{0,64},{64,128},{128,192},{192,256},{256,320},{320,384},{384,448},... | collective-permute-start | bytes 786440 | tf_op jit(solution)/shard_map/while/body/eval_jaxpr/ppermute | solution.py:34
  265.6 9.7 %collective-permute-start.5 = (f32[2,16,2048]{2,1,0:T(8,128)S(1)}, f32[2,16,2048]{2,1,0:T(8,128)}, u32[]{:S(2)}, u32[]{:S(2)}) collective-permute-start(f32[2,16,2048]{2,1,0:T(8,128)S(1)} %get-tuple-element.1672), channel_id=1, source_target_pairs={{0,64},{64,128},{128,192},{192,256},{256,320},{320,384},{384,448},... | collective-permute-start | bytes 786440 | tf_op jit(solution)/shard_map/while/body/eval_jaxpr/ppermute | solution.py:34
  309.6 9.7 %collective-permute-start.5 = (f32[2,16,2048]{2,1,0:T(8,128)S(1)}, f32[2,16,2048]{2,1,0:T(8,128)}, u32[]{:S(2)}, u32[]{:S(2)}) collective-permute-start(f32[2,16,2048]{2,1,0:T(8,128)S(1)} %get-tuple-element.1672), channel_id=1, source_target_pairs={{0,64},{64,128},{128,192},{192,256},{256,320},{320,384},{384,448},... | collective-permute-start | bytes 786440 | tf_op jit(solution)/shard_map/while/body/eval_jaxpr/ppermute | solution.py:34
  353.5 9.7 %collective-permute-start.5 = (f32[2,16,2048]{2,1,0:T(8,128)S(1)}, f32[2,16,2048]{2,1,0:T(8,128)}, u32[]{:S(2)}, u32[]{:S(2)}) collective-permute-start(f32[2,16,2048]{2,1,0:T(8,128)S(1)} %get-tuple-element.1672), channel_id=1, source_target_pairs={{0,64},{64,128},{128,192},{192,256},{256,320},{320,384},{384,448},... | collective-permute-start | bytes 786440 | tf_op jit(solution)/shard_map/while/body/eval_jaxpr/ppermute | solution.py:34
  368.4 9.4 %collective-permute-start = (f32[16,16,16]{2,0,1:T(8,128)S(1)}, f32[16,16,16]{2,0,1:T(8,128)S(1)}, u32[]{:S(2)}, u32[]{:S(2)}) collective-permute-start(f32[16,16,16]{2,0,1:T(8,128)S(1)} %get-tuple-element.1708), channel_id=1, source_target_pairs={{0,1},{1,2},{2,3},{3,4},{4,5},{5,6},{6,7},{7,8},{8,9},{9,10},{10,1... | collective-permute-start | bytes 49160 | tf_op jit(solution)/shard_map/while/body/eval_jaxpr/while/body/eval_jaxpr/ppermute | solution.py:22
  384.0 9.3 %collective-permute-start = (f32[16,16,16]{2,0,1:T(8,128)S(1)}, f32[16,16,16]{2,0,1:T(8,128)S(1)}, u32[]{:S(2)}, u32[]{:S(2)}) collective-permute-start(f32[16,16,16]{2,0,1:T(8,128)S(1)} %get-tuple-element.1708), channel_id=1, source_target_pairs={{0,1},{1,2},{2,3},{3,4},{4,5},{5,6},{6,7},{7,8},{8,9},{9,10},{10,1... | collective-permute-start | bytes 49160 | tf_op jit(solution)/shard_map/while/body/eval_jaxpr/while/body/eval_jaxpr/ppermute | solution.py:22
  396.6 10.2 %collective-permute-start.2 = (f32[2,16,2048]{2,1,0:T(8,128)S(1)}, f32[2,16,2048]{2,1,0:T(8,128)S(1)}, u32[]{:S(2)}, u32[]{:S(2)}) collective-permute-start(f32[2,16,2048]{2,1,0:T(8,128)S(1)} %get-tuple-element.1689), channel_id=1, source_target_pairs={{64,0},{128,64},{192,128},{256,192},{320,256},{384,320},{448,384},... | collective-permute-start | bytes 786440 | tf_op jit(solution)/shard_map/while/body/eval_jaxpr/ppermute | solution.py:34
  411.1 10.1 %collective-permute-start = (f32[16,16,16]{2,0,1:T(8,128)S(1)}, f32[16,16,16]{2,0,1:T(8,128)S(1)}, u32[]{:S(2)}, u32[]{:S(2)}) collective-permute-start(f32[16,16,16]{2,0,1:T(8,128)S(1)} %get-tuple-element.1708), channel_id=1, source_target_pairs={{0,1},{1,2},{2,3},{3,4},{4,5},{5,6},{6,7},{7,8},{8,9},{9,10},{10,1... | collective-permute-start | bytes 49160 | tf_op jit(solution)/shard_map/while/body/eval_jaxpr/while/body/eval_jaxpr/ppermute | solution.py:22
  427.3 9.9 %collective-permute-start = (f32[16,16,16]{2,0,1:T(8,128)S(1)}, f32[16,16,16]{2,0,1:T(8,128)S(1)}, u32[]{:S(2)}, u32[]{:S(2)}) collective-permute-start(f32[16,16,16]{2,0,1:T(8,128)S(1)} %get-tuple-element.1708), channel_id=1, source_target_pairs={{0,1},{1,2},{2,3},{3,4},{4,5},{5,6},{6,7},{7,8},{8,9},{9,10},{10,1... | collective-permute-start | bytes 49160 | tf_op jit(solution)/shard_map/while/body/eval_jaxpr/while/body/eval_jaxpr/ppermute | solution.py:22
  429.3 8.9 %collective-permute-start.1 = (f32[16,16,16]{2,0,1:T(8,128)S(1)}, f32[16,16,16]{2,0,1:T(8,128)S(1)}, u32[]{:S(2)}, u32[]{:S(2)}) collective-permute-start(f32[16,16,16]{2,0,1:T(8,128)S(1)} %get-tuple-element.1709), channel_id=1, source_target_pairs={{1,0},{2,1},{3,2},{4,3},{5,4},{6,5},{7,6},{8,7},{9,8},{10,9},{11,1... | collective-permute-start | bytes 49160 | tf_op jit(solution)/shard_map/while/body/eval_jaxpr/while/body/eval_jaxpr/ppermute | solution.py:24
  453.0 10.1 %collective-permute-start = (f32[16,16,16]{2,0,1:T(8,128)S(1)}, f32[16,16,16]{2,0,1:T(8,128)S(1)}, u32[]{:S(2)}, u32[]{:S(2)}) collective-permute-start(f32[16,16,16]{2,0,1:T(8,128)S(1)} %get-tuple-element.1708), channel_id=1, source_target_pairs={{0,1},{1,2},{2,3},{3,4},{4,5},{5,6},{6,7},{7,8},{8,9},{9,10},{10,1... | collective-permute-start | bytes 49160 | tf_op jit(solution)/shard_map/while/body/eval_jaxpr/while/body/eval_jaxpr/ppermute | solution.py:22
  469.3 9.9 %collective-permute-start = (f32[16,16,16]{2,0,1:T(8,128)S(1)}, f32[16,16,16]{2,0,1:T(8,128)S(1)}, u32[]{:S(2)}, u32[]{:S(2)}) collective-permute-start(f32[16,16,16]{2,0,1:T(8,128)S(1)} %get-tuple-element.1708), channel_id=1, source_target_pairs={{0,1},{1,2},{2,3},{3,4},{4,5},{5,6},{6,7},{7,8},{8,9},{9,10},{10,1... | collective-permute-start | bytes 49160 | tf_op jit(solution)/shard_map/while/body/eval_jaxpr/while/body/eval_jaxpr/ppermute | solution.py:22
  495.0 10.1 %collective-permute-start = (f32[16,16,16]{2,0,1:T(8,128)S(1)}, f32[16,16,16]{2,0,1:T(8,128)S(1)}, u32[]{:S(2)}, u32[]{:S(2)}) collective-permute-start(f32[16,16,16]{2,0,1:T(8,128)S(1)} %get-tuple-element.1708), channel_id=1, source_target_pairs={{0,1},{1,2},{2,3},{3,4},{4,5},{5,6},{6,7},{7,8},{8,9},{9,10},{10,1... | collective-permute-start | bytes 49160 | tf_op jit(solution)/shard_map/while/body/eval_jaxpr/while/body/eval_jaxpr/ppermute | solution.py:22
  511.3 9.9 %collective-permute-start = (f32[16,16,16]{2,0,1:T(8,128)S(1)}, f32[16,16,16]{2,0,1:T(8,128)S(1)}, u32[]{:S(2)}, u32[]{:S(2)}) collective-permute-start(f32[16,16,16]{2,0,1:T(8,128)S(1)} %get-tuple-element.1708), channel_id=1, source_target_pairs={{0,1},{1,2},{2,3},{3,4},{4,5},{5,6},{6,7},{7,8},{8,9},{9,10},{10,1... | collective-permute-start | bytes 49160 | tf_op jit(solution)/shard_map/while/body/eval_jaxpr/while/body/eval_jaxpr/ppermute | solution.py:22
  513.2 8.9 %collective-permute-start.1 = (f32[16,16,16]{2,0,1:T(8,128)S(1)}, f32[16,16,16]{2,0,1:T(8,128)S(1)}, u32[]{:S(2)}, u32[]{:S(2)}) collective-permute-start(f32[16,16,16]{2,0,1:T(8,128)S(1)} %get-tuple-element.1709), channel_id=1, source_target_pairs={{1,0},{2,1},{3,2},{4,3},{5,4},{6,5},{7,6},{8,7},{9,8},{10,9},{11,1... | collective-permute-start | bytes 49160 | tf_op jit(solution)/shard_map/while/body/eval_jaxpr/while/body/eval_jaxpr/ppermute | solution.py:24
  536.9 10.1 %collective-permute-start = (f32[16,16,16]{2,0,1:T(8,128)S(1)}, f32[16,16,16]{2,0,1:T(8,128)S(1)}, u32[]{:S(2)}, u32[]{:S(2)}) collective-permute-start(f32[16,16,16]{2,0,1:T(8,128)S(1)} %get-tuple-element.1708), channel_id=1, source_target_pairs={{0,1},{1,2},{2,3},{3,4},{4,5},{5,6},{6,7},{7,8},{8,9},{9,10},{10,1... | collective-permute-start | bytes 49160 | tf_op jit(solution)/shard_map/while/body/eval_jaxpr/while/body/eval_jaxpr/ppermute | solution.py:22
  553.3 9.9 %collective-permute-start = (f32[16,16,16]{2,0,1:T(8,128)S(1)}, f32[16,16,16]{2,0,1:T(8,128)S(1)}, u32[]{:S(2)}, u32[]{:S(2)}) collective-permute-start(f32[16,16,16]{2,0,1:T(8,128)S(1)} %get-tuple-element.1708), channel_id=1, source_target_pairs={{0,1},{1,2},{2,3},{3,4},{4,5},{5,6},{6,7},{7,8},{8,9},{9,10},{10,1... | collective-permute-start | bytes 49160 | tf_op jit(solution)/shard_map/while/body/eval_jaxpr/while/body/eval_jaxpr/ppermute | solution.py:22
  555.2 8.9 %collective-permute-start.1 = (f32[16,16,16]{2,0,1:T(8,128)S(1)}, f32[16,16,16]{2,0,1:T(8,128)S(1)}, u32[]{:S(2)}, u32[]{:S(2)}) collective-permute-start(f32[16,16,16]{2,0,1:T(8,128)S(1)} %get-tuple-element.1709), channel_id=1, source_target_pairs={{1,0},{2,1},{3,2},{4,3},{5,4},{6,5},{7,6},{8,7},{9,8},{10,9},{11,1... | collective-permute-start | bytes 49160 | tf_op jit(solution)/shard_map/while/body/eval_jaxpr/while/body/eval_jaxpr/ppermute | solution.py:24
  579.0 10.1 %collective-permute-start = (f32[16,16,16]{2,0,1:T(8,128)S(1)}, f32[16,16,16]{2,0,1:T(8,128)S(1)}, u32[]{:S(2)}, u32[]{:S(2)}) collective-permute-start(f32[16,16,16]{2,0,1:T(8,128)S(1)} %get-tuple-element.1708), channel_id=1, source_target_pairs={{0,1},{1,2},{2,3},{3,4},{4,5},{5,6},{6,7},{7,8},{8,9},{9,10},{10,1... | collective-permute-start | bytes 49160 | tf_op jit(solution)/shard_map/while/body/eval_jaxpr/while/body/eval_jaxpr/ppermute | solution.py:22
  595.3 9.8 %collective-permute-start = (f32[16,16,16]{2,0,1:T(8,128)S(1)}, f32[16,16,16]{2,0,1:T(8,128)S(1)}, u32[]{:S(2)}, u32[]{:S(2)}) collective-permute-start(f32[16,16,16]{2,0,1:T(8,128)S(1)} %get-tuple-element.1708), channel_id=1, source_target_pairs={{0,1},{1,2},{2,3},{3,4},{4,5},{5,6},{6,7},{7,8},{8,9},{9,10},{10,1... | collective-permute-start | bytes 49160 | tf_op jit(solution)/shard_map/while/body/eval_jaxpr/while/body/eval_jaxpr/ppermute | solution.py:22
  597.2 8.9 %collective-permute-start.1 = (f32[16,16,16]{2,0,1:T(8,128)S(1)}, f32[16,16,16]{2,0,1:T(8,128)S(1)}, u32[]{:S(2)}, u32[]{:S(2)}) collective-permute-start(f32[16,16,16]{2,0,1:T(8,128)S(1)} %get-tuple-element.1709), channel_id=1, source_target_pairs={{1,0},{2,1},{3,2},{4,3},{5,4},{6,5},{7,6},{8,7},{9,8},{10,9},{11,1... | collective-permute-start | bytes 49160 | tf_op jit(solution)/shard_map/while/body/eval_jaxpr/while/body/eval_jaxpr/ppermute | solution.py:24
  621.0 10.1 %collective-permute-start = (f32[16,16,16]{2,0,1:T(8,128)S(1)}, f32[16,16,16]{2,0,1:T(8,128)S(1)}, u32[]{:S(2)}, u32[]{:S(2)}) collective-permute-start(f32[16,16,16]{2,0,1:T(8,128)S(1)} %get-tuple-element.1708), channel_id=1, source_target_pairs={{0,1},{1,2},{2,3},{3,4},{4,5},{5,6},{6,7},{7,8},{8,9},{9,10},{10,1... | collective-permute-start | bytes 49160 | tf_op jit(solution)/shard_map/while/body/eval_jaxpr/while/body/eval_jaxpr/ppermute | solution.py:22
  637.3 9.6 %collective-permute-start = (f32[16,16,16]{2,0,1:T(8,128)S(1)}, f32[16,16,16]{2,0,1:T(8,128)S(1)}, u32[]{:S(2)}, u32[]{:S(2)}) collective-permute-start(f32[16,16,16]{2,0,1:T(8,128)S(1)} %get-tuple-element.1708), channel_id=1, source_target_pairs={{0,1},{1,2},{2,3},{3,4},{4,5},{5,6},{6,7},{7,8},{8,9},{9,10},{10,1... | collective-permute-start | bytes 49160 | tf_op jit(solution)/shard_map/while/body/eval_jaxpr/while/body/eval_jaxpr/ppermute | solution.py:22
  639.3 8.9 %collective-permute-start.1 = (f32[16,16,16]{2,0,1:T(8,128)S(1)}, f32[16,16,16]{2,0,1:T(8,128)S(1)}, u32[]{:S(2)}, u32[]{:S(2)}) collective-permute-start(f32[16,16,16]{2,0,1:T(8,128)S(1)} %get-tuple-element.1709), channel_id=1, source_target_pairs={{1,0},{2,1},{3,2},{4,3},{5,4},{6,5},{7,6},{8,7},{9,8},{10,9},{11,1... | collective-permute-start | bytes 49160 | tf_op jit(solution)/shard_map/while/body/eval_jaxpr/while/body/eval_jaxpr/ppermute | solution.py:24
  663.1 10.1 %collective-permute-start = (f32[16,16,16]{2,0,1:T(8,128)S(1)}, f32[16,16,16]{2,0,1:T(8,128)S(1)}, u32[]{:S(2)}, u32[]{:S(2)}) collective-permute-start(f32[16,16,16]{2,0,1:T(8,128)S(1)} %get-tuple-element.1708), channel_id=1, source_target_pairs={{0,1},{1,2},{2,3},{3,4},{4,5},{5,6},{6,7},{7,8},{8,9},{9,10},{10,1... | collective-permute-start | bytes 49160 | tf_op jit(solution)/shard_map/while/body/eval_jaxpr/while/body/eval_jaxpr/ppermute | solution.py:22
  679.4 9.5 %collective-permute-start = (f32[16,16,16]{2,0,1:T(8,128)S(1)}, f32[16,16,16]{2,0,1:T(8,128)S(1)}, u32[]{:S(2)}, u32[]{:S(2)}) collective-permute-start(f32[16,16,16]{2,0,1:T(8,128)S(1)} %get-tuple-element.1708), channel_id=1, source_target_pairs={{0,1},{1,2},{2,3},{3,4},{4,5},{5,6},{6,7},{7,8},{8,9},{9,10},{10,1... | collective-permute-start | bytes 49160 | tf_op jit(solution)/shard_map/while/body/eval_jaxpr/while/body/eval_jaxpr/ppermute | solution.py:22
  681.3 8.9 %collective-permute-start.1 = (f32[16,16,16]{2,0,1:T(8,128)S(1)}, f32[16,16,16]{2,0,1:T(8,128)S(1)}, u32[]{:S(2)}, u32[]{:S(2)}) collective-permute-start(f32[16,16,16]{2,0,1:T(8,128)S(1)} %get-tuple-element.1709), channel_id=1, source_target_pairs={{1,0},{2,1},{3,2},{4,3},{5,4},{6,5},{7,6},{8,7},{9,8},{10,9},{11,1... | collective-permute-start | bytes 49160 | tf_op jit(solution)/shard_map/while/body/eval_jaxpr/while/body/eval_jaxpr/ppermute | solution.py:24
  (211 other events, 1052.5 us)
where the time goes:
time: 710 us; the launch traced here: 701 us
  starting transfers between devices  292 us (41%)
  matrix products  148 us (21%)
  local copies, waits for them, and re-layouts  125 us (18%)
  waiting for transfers between devices  67.1 us (9%)
  other arithmetic  61.6 us (9%)
    ppermute x32, starting transfers between devices, with_halo(): lax.ppermute(head, axis, [((i + 1) % count, i) for i in range(ends)])  142 us
    dot_general x144, matrix products, matmul(): return jnp.dot(left, right, precision=HIGH)  89.2 us
    ppermute x32, starting transfers between devices, with_halo(): lax.ppermute(tail, axis, [(i, (i + 1) % count) for i in range(ends)])  76.8 us
    ppermute x16, starting transfers between devices, passed_along(): lax.ppermute(value, axis, [(source, source + steps) for source in range(l...  73.1 us
    scatter-add x32, local copies, waits for them, and re-layouts, level(): own = own.at[:, :, TILE - HALO:].add(returned[:, :, 3 * HALO:])  40.8 us
    dot_general x16, matrix products, level(): jnp.einsum('fck,cjk->fcj', extended, picker, precision=HIGH)  39.4 us
    ppermute x16, waiting for transfers between devices, passed_along(): lax.ppermute(value, axis, [(source, source + steps) for source in range(l...  32.9 us
    dynamic_slice x32, local copies, waits for them, and re-layouts, sweep_forward(): lax.scan(level, inbound, (base, flux, pore_mask, upwind, side_link))  32.9 us
  transfers between devices with their start and end apart: 80, of which 44 were waited for; matrix products, arithmetic and copies ran while one was open for 18% of the time, Pallas kernels for 0%

commit v1 on v0

v1 whole, which is shorter than its diff:
```python
import jax
import jax.numpy as jnp
from jax import lax
from jax.experimental import pallas as pl
from jax.experimental.pallas import tpu as pltpu
from jax.sharding import PartitionSpec as P

FACE = 16
TILE = 128
HALO = 16
LEVELS_HERE = 2
GROUP = 4
HALF = TILE // 2
BOTH = 2 * FACE
NEAR = 3 * FACE

HIGH = lax.Precision.HIGHEST
F32 = jnp.float32
BF16 = jnp.bfloat16
MESH = pl.DeviceIdType.MESH


def halves(value):
    high = value.astype(BF16)
    low = (value - high.astype(F32)).astype(BF16)
    return high, low


def stacked(value):
    high, low = halves(value)
    return jnp.concatenate([high, low, high], axis=0)


def product(left, right):
    return jnp.dot(left, right, preferred_element_type=F32)


def cross_product(left, right):
    return lax.dot_general(left, right, (((1,), (1,)), ((), ())), preferred_element_type=F32)


def widened(weight, wide, target):
    depth = weight.shape[1]
    high = weight.astype(BF16).astype(F32)
    wide[0 : weight.shape[0], 0:depth] = high
    wide[0 : weight.shape[0], depth : 2 * depth] = high
    wide[0 : weight.shape[0], 2 * depth : 3 * depth] = weight - high
    target[...] = wide[0 : weight.shape[0], 0 : 3 * depth].astype(BF16)


def kernel(
    source,
    cotangent,
    flux,
    pore_mask,
    upwind,
    side_link,
    local_inverse,
    flow_lift,
    side_lift,
    flow_trace,
    side_trace,
    concentration,
    sensitivity,
    field,
    lead,
    scale,
    pick,
    pick_beside,
    pick_next,
    kept,
    late,
    main_in,
    main_out,
    near_out,
    near_left,
    near_right,
    far_left,
    far_right,
    fix_out,
    fix_left,
    fix_right,
    fact_out,
    fact_left,
    fact_right,
    fact_next,
    start_out,
    start_left,
    start_right,
    lift,
    wide,
    local_weight,
    chain_weight,
    out_weight,
    field_sem,
    done_sem,
    main_sem,
    near_sem,
    far_sem,
    fix_sem,
    fact_sem,
    next_sem,
    start_sem,
):
    flow_count = lax.axis_size("flow")
    cross_count = lax.axis_size("cross")
    place = lax.axis_index("flow")
    block = lax.axis_index("cross")
    pieces = main_in.shape[1]
    whole_width = main_in.shape[3]
    width = whole_width - TILE
    nodes = field.shape[2]
    inputs = (source, cotangent)
    results = (concentration, sensitivity)
    is_first = (place == 0, place == flow_count - 1)
    is_last = (place == flow_count - 1, place == 0)
    downstream = (place + 1, place - 1)
    below, above = place > 0, place < flow_count - 1

    def beside(steps):
        return lax.rem(block + cross_count + steps, cross_count)

    def loaded(sweep):
        return pltpu.make_async_copy(inputs[sweep], field.at[sweep], field_sem.at[sweep])

    loaded(0).start()
    loaded(1).start()

    barrier = pltpu.get_barrier_semaphore()

    def greet(flow_at, steps):
        pl.semaphore_signal(
            barrier, inc=1, device_id=(flow_at, beside(steps)), device_id_type=MESH
        )

    greet(place, -1)
    greet(place, 1)

    @pl.when(below)
    def _():
        for steps in range(-2, 3):
            greet(place - 1, steps)

    @pl.when(above)
    def _():
        for steps in range(-2, 3):
            greet(place + 1, steps)

    inverse = local_inverse[...]
    lift[:, 0:FACE] = flow_lift[...]
    lift[:, FACE:BOTH] = side_lift[...]
    lifts = lift[...]
    trace = jnp.concatenate([flow_trace[...], side_trace[...]], axis=0)
    traced_inverse = jnp.dot(trace, inverse, precision=HIGH, preferred_element_type=F32)
    traced_lift = jnp.dot(trace, lifts, precision=HIGH, preferred_element_type=F32)
    widened(jnp.concatenate([inverse, traced_inverse], axis=0), wide, local_weight.at[0])
    widened(jnp.concatenate([inverse.T, lifts.T], axis=0), wide, local_weight.at[1])
    widened(traced_lift, wide, chain_weight.at[0])
    widened(traced_lift.T, wide, chain_weight.at[1])
    widened(lifts, wide, out_weight.at[0])
    widened(traced_inverse.T, wide, out_weight.at[1])

    def lanes(rows):
        return lax.broadcasted_iota(jnp.int32, (rows, TILE), 1)

    def packed(value):
        lane = lanes(value.shape[0])
        edge = jnp.zeros(lane.shape, F32)
        for at in range(GROUP):
            tile = value[:, at * TILE : (at + 1) * TILE]
            start = at * HALO
            tail = pltpu.roll(tile, (start + HALO) % TILE, 1)
            head = pltpu.roll(tile, (start + HALF) % TILE, 1)
            edge = jnp.where((lane >= start) & (lane < start + HALO), tail, edge)
            edge = jnp.where((lane >= start + HALF) & (lane < start + HALF + HALO), head, edge)
        return edge

    def unpacked(edge, at):
        lane = lanes(edge.shape[0])
        start = at * HALO
        head = pltpu.roll(edge, (TILE - HALF - start) % TILE, 1)
        tail = pltpu.roll(edge, (TILE - HALO - start) % TILE, 1)
        return jnp.where(lane < HALO, head, jnp.where(lane >= TILE - HALO, tail, 0.0))

    def is_open(reach):
        return (
            (block >= reach).astype(jnp.int32),
            (block < cross_count - reach).astype(jnp.int32),
        )

    def inward(from_left, from_right, reach=1):
        lane = lanes(from_left.shape[0])
        opened = jnp.where(lane < HALF, *is_open(reach))
        return jnp.where(opened > 0, jnp.where(lane < HALF, from_left, from_right), 0.0)

    def homeward(from_left, from_right, reach=1):
        lane = lanes(from_left.shape[0])
        opened = jnp.where(lane < HALF, *is_open(reach)[::-1])
        return jnp.where(opened > 0, jnp.where(lane < HALF, from_right, from_left), 0.0)

    def columns_of(piece):
        return pl.ds(pl.multiple_of(piece * width, width), width)

    def live(level, piece):
        return pore_mask[level : level + 1, columns_of(piece)].astype(F32)

    def codes(level, piece):
        cols = columns_of(piece)
        inflow = upwind[level : level + 1, cols]
        return jnp.where(inflow != 0, side_link[level : level + 1, cols], -1)

    def gather_facts(piece, carry):
        for level in range(LEVELS_HERE):
            cols = columns_of(piece)
            scale[level, piece, :, 0:width] = live(level, piece) * flux[level : level + 1, cols]
        rows = jnp.concatenate(
            [
                scale[0, piece, :, 0:width],
                codes(0, piece).astype(F32),
                jnp.zeros((6, width), F32),
            ],
            axis=0,
        )
        fact_out[piece] = packed(rows)
        return carry

    lax.fori_loop(0, pieces, gather_facts, 0)

    def send(src, dst, send_sem, recv_sem, flow_at, steps):
        return pltpu.make_async_remote_copy(
            src_ref=src,
            dst_ref=dst,
            send_sem=send_sem,
            recv_sem=recv_sem,
            device_id=(flow_at, beside(steps)),
            device_id_type=MESH,
        )

    def pair(src, at_left, at_right, sem, flow_at, reach=1):
        return (
            send(src, at_left, sem(0), sem(1), flow_at, reach),
            send(src, at_right, sem(2), sem(3), flow_at, -reach),
        )

    def fact_copies():
        return pair(fact_out, fact_left, fact_right, lambda n: fact_sem.at[n], place)

    def next_copy():
        return send(fact_out, fact_next, next_sem.at[0], next_sem.at[1], place - 1, 0)

    def start_copies():
        return pair(start_out, start_left, start_right, lambda n: start_sem.at[n], place)

    def fix_copies(piece):
        return pair(
            fix_out.at[piece],
            fix_left.at[piece],
            fix_right.at[piece],
            lambda n: fix_sem.at[n, piece],
            place,
        )

    def wave_copies(sweep, piece):
        flow_at = downstream[sweep]
        main = send(
            main_out.at[sweep, piece],
            main_in.at[sweep, piece],
            main_sem.at[0, sweep, piece],
            main_sem.at[1, sweep, piece],
            flow_at,
            0,
        )
        near = pair(
            near_out.at[sweep, piece, pl.ds(0, NEAR)],
            near_left.at[sweep, piece],
            near_right.at[sweep, piece],
            lambda n: near_sem.at[n, sweep, piece],
            flow_at,
        )
        far = pair(
            near_out.at[sweep, piece, pl.ds(NEAR, FACE)],
            far_left.at[sweep, piece],
            far_right.at[sweep, piece],
            lambda n: far_sem.at[n, sweep, piece],
            flow_at,
            2,
        )
        return near + far + (main,)

    pl.semaphore_wait(barrier, 2 + 5 * below.astype(jnp.int32) + 5 * above.astype(jnp.int32))

    for copy in fact_copies():
        copy.start()

    @pl.when(below)
    def _():
        next_copy().start()

    def one_hot(row, depth):
        rows = lax.broadcasted_iota(jnp.int32, (depth, TILE), 0)
        return jnp.where(rows == row, 1.0, 0.0).astype(BF16)

    def build_pick(piece, carry):
        for level in range(LEVELS_HERE):
            code = codes(level, piece)
            for at in range(GROUP):
                link = code[:, at * TILE : (at + 1) * TILE]
                row = jnp.where(
                    link < HALO,
                    link + (TILE + at * HALO),
                    jnp.where(
                        link < HALO + TILE, link - HALO, link + (HALF + at * HALO - HALO)
                    ),
                )
                row = jnp.where(link >= 0, row, -1)
                pick[level, piece * GROUP + at] = one_hot(row, 2 * TILE)
        return carry

    lax.fori_loop(0, pieces, build_pick, 0)

    def settle_facts():
        for copy in fact_copies():
            copy.wait_recv()

        @pl.when(above)
        def _():
            next_copy().wait_recv()

        @pl.when(jnp.logical_not(above))
        def _():
            fact_next[...] = jnp.zeros(fact_next.shape, F32)

        lane = lanes(1)
        start = lax.rem(lane, HALF) // HALO * HALO
        on_left = lane < HALF

        def one(piece, carry):
            facts = inward(fact_left[piece], fact_right[piece])
            scale[0, piece, :, width:whole_width] = facts[0:1]
            link = facts[1:2].astype(jnp.int32)
            low = (link >= 0) & (link < HALO)
            high = link >= HALO + TILE
            after = link - (HALO + TILE)
            left_row = jnp.where(
                high, HALF + start + after, jnp.where(low, TILE + start + link, -1)
            )
            right_row = jnp.where(
                low, start + link, jnp.where(high, TILE + HALF + start + after, -1)
            )
            pick_beside[piece] = one_hot(jnp.where(on_left, left_row, right_row), 2 * TILE)
            link = fact_next[piece][1:2].astype(jnp.int32)
            inside = (link >= HALO) & (link < HALO + TILE)
            row = jnp.where(inside, start * (TILE // HALO) + link - HALO, -1)
            pick_next[piece] = one_hot(row, width)
            return carry

        lax.fori_loop(0, pieces, one, 0)

    def prepare(sweep):
        loaded(sweep).wait()

        def one(level, piece):
            cols = columns_of(piece)
            value = product(local_weight[sweep], stacked(field[sweep, level, :, cols]))
            mask = live(level, piece)
            field[sweep, level, :, cols] = mask * value[:nodes]
            added = (mask if sweep == 0 else scale[level, piece, :, 0:width]) * value[nodes:]
            lead[sweep, level, piece, :, 0:width] = added
            if level == 0:
                lead[sweep, 0, piece, :, width:whole_width] = jnp.zeros((BOTH, TILE), F32)
                if sweep == 0:
                    start_out[piece] = packed(added[FACE:])

        def first_level(piece, carry):
            one(0, piece)
            return carry

        def second_level(piece, carry):
            one(1, piece)
            return carry

        lax.fori_loop(0, pieces, first_level, 0)
        if sweep == 0:
            for copy in start_copies():
                copy.start()
        lax.fori_loop(0, pieces, second_level, 0)

    def arrive(sweep, piece):
        @pl.when(is_first[sweep])
        def _():
            main_in[sweep, piece] = jnp.zeros((BOTH, whole_width), F32)
            near_left[sweep, piece] = jnp.zeros((NEAR, TILE), F32)
            near_right[sweep, piece] = jnp.zeros((NEAR, TILE), F32)
            far_left[sweep, piece] = jnp.zeros((FACE, TILE), F32)
            far_right[sweep, piece] = jnp.zeros((FACE, TILE), F32)

        @pl.when(jnp.logical_not(is_first[sweep]))
        def _():
            for copy in wave_copies(sweep, piece):
                copy.wait_recv()

    def leave(sweep, piece):
        for copy in wave_copies(sweep, piece):
            copy.start()

    def picked(near, beyond, one_hots):
        near_high, near_low = near
        beyond_high, beyond_low = beyond
        extended = jnp.concatenate(
            [
                jnp.concatenate([near_high, beyond_high], axis=1),
                jnp.concatenate([near_low, beyond_low], axis=1),
            ],
            axis=0,
        )
        value = product(extended, one_hots)
        return value[:FACE] + value[FACE:]

    def spread(value, one_hots):
        value = cross_product(jnp.concatenate(halves(value), axis=0), one_hots)
        return value[:FACE] + value[FACE:]

    def cut(value, at):
        return value[:, at * TILE : (at + 1) * TILE]

    def gathered(sides, halo, level, piece):
        halo = halves(halo)
        high, low = halves(sides)
        return [
            picked((cut(high, at), cut(low, at)), halo, pick[level, piece * GROUP + at])
            for at in range(GROUP)
        ]

    def scattered(sides, level, piece):
        own = []
        edge = jnp.zeros((FACE, TILE), F32)
        for at in range(GROUP):
            value = spread(cut(sides, at), pick[level, piece * GROUP + at])
            own.append(value[:, :TILE])
            edge = edge + value[:, TILE:]
        return own, edge

    def forward(piece):
        arrive(0, piece)
        main = main_in[0, piece]
        near = inward(near_left[0, piece], near_right[0, piece])
        outer = inward(far_left[0, piece], far_right[0, piece], 2)
        sides = gathered(main[FACE:, :width], near[BOTH:], 0, piece)
        sides.append(
            near[FACE:BOTH]
            + picked(halves(main[FACE:, width:]), halves(outer), pick_beside[piece])
        )
        inbound = jnp.concatenate(
            [
                jnp.concatenate([main[:FACE, :width], near[:FACE]], axis=1),
                jnp.concatenate(sides, axis=1),
            ],
            axis=0,
        )
        operand = stacked(inbound)
        kept[0, 0, piece] = operand[:, :width]
        value = lead[0, 0, piece] + scale[0, piece] * product(chain_weight[0], operand)
        sides = gathered(value[FACE:, :width], value[FACE:, width:], 1, piece)
        operand = stacked(
            jnp.concatenate([value[:FACE, :width], jnp.concatenate(sides, axis=1)], axis=0)
        )
        kept[0, 1, piece] = operand

        @pl.when(jnp.logical_not(is_last[0]))
        def _():
            value = lead[0, 1, piece, :, 0:width] + scale[1, piece, :, 0:width] * product(
                chain_weight[0], operand
            )
            edges = packed(value)
            ahead = product(jnp.concatenate(halves(value[FACE:]), axis=0), pick_next[piece])
            main_out[0, piece, :, 0:width] = value
            main_out[0, piece, :, width:whole_width] = edges
            near_out[0, piece, 0:FACE] = edges[:FACE]
            near_out[0, piece, FACE:BOTH] = ahead[:FACE] + ahead[FACE:]
            near_out[0, piece, BOTH:NEAR] = edges[FACE:]
            near_out[0, piece, NEAR : NEAR + FACE] = edges[FACE:]
            leave(0, piece)

    def adjoint(piece):
        arrive(1, piece)
        main = main_in[1, piece]
        near = homeward(near_left[1, piece], near_right[1, piece])
        outer = homeward(far_left[1, piece], far_right[1, piece], 2)
        edges = jnp.concatenate(
            [near[:FACE], main[FACE:, width:] + near[BOTH:] + outer], axis=0
        )
        behind = spread(near[FACE:BOTH], pick_next[piece])
        none = jnp.zeros((FACE, TILE), F32)
        inbound = jnp.concatenate(
            [
                cut(main, at)
                + unpacked(edges, at)
                + jnp.concatenate([none, cut(behind, at)], axis=0)
                for at in range(GROUP)
            ],
            axis=1,
        )
        operand = stacked(inbound)
        kept[1, 1, piece] = operand
        value = lead[1, 1, piece, :, 0:width] + scale[1, piece, :, 0:width] * product(
            chain_weight[1], operand
        )
        own, edge = scattered(value[FACE:], 1, piece)
        fix_out[piece] = edge
        for copy in fix_copies(piece):
            copy.start()
        inbound = jnp.concatenate(
            [
                jnp.concatenate([value[:FACE], none], axis=1),
                jnp.concatenate(own + [edge], axis=1),
            ],
            axis=0,
        )
        late[piece] = inbound[:, :width]

        @pl.when(jnp.logical_not(is_last[1]))
        def _():
            value = lead[1, 0, piece] + scale[0, piece] * product(
                chain_weight[1], stacked(inbound)
            )
            own, edge = scattered(value[FACE:, :width], 0, piece)
            around = spread(value[FACE:, width:], pick_beside[piece])
            own.append(around[:, :TILE])
            main_out[1, piece, 0:FACE] = jnp.concatenate([value[:FACE, :width], none], axis=1)
            main_out[1, piece, FACE:BOTH] = jnp.concatenate(own, axis=1)
            near_out[1, piece, 0:BOTH] = value[:, width:]
            near_out[1, piece, BOTH:NEAR] = edge
            near_out[1, piece, NEAR : NEAR + FACE] = around[:, TILE:]
            leave(1, piece)

    def written(sweep, piece):
        cols = columns_of(piece)
        return pltpu.make_async_copy(
            field.at[sweep, :, :, cols], results[sweep].at[:, :, cols], done_sem.at[sweep, piece]
        )

    def finish(sweep, piece):
        cols = columns_of(piece)
        for level in range(LEVELS_HERE):
            if sweep == 1 and level == 0:
                for copy in fix_copies(piece):
                    copy.wait_recv()
                edges = homeward(fix_left[piece], fix_right[piece])
                sides = [
                    cut(late[piece, FACE:BOTH], at) + unpacked(edges, at) for at in range(GROUP)
                ]
                operand = stacked(
                    jnp.concatenate(
                        [late[piece, 0:FACE], jnp.concatenate(sides, axis=1)], axis=0
                    )
                )
            else:
                operand = kept[sweep, level, piece]
            factor = scale[level, piece, :, 0:width] if sweep == 0 else live(level, piece)
            field[sweep, level, :, cols] += factor * product(out_weight[sweep], operand)
        written(sweep, piece).start()

    def chain(sweep):
        step = forward if sweep == 0 else adjoint
        if sweep == 0:
            for copy in start_copies():
                copy.wait_recv()

            def begin(piece, carry):
                lead[0, 0, piece, FACE:BOTH, width:whole_width] = inward(
                    start_left[piece], start_right[piece]
                )
                return carry

            lax.fori_loop(0, pieces, begin, 0)

        def one(piece, carry):
            step(piece)
            return carry

        def last(piece, carry):
            finish(sweep, piece)
            return carry

        lax.fori_loop(0, pieces, one, 0)
        lax.fori_loop(0, pieces, last, 0)

    first = (place >= flow_count // 2).astype(jnp.int32)
    on_end = jnp.logical_or(place == 0, place == flow_count - 1)

    def slot(at, carry):
        early = jnp.where(on_end, 2 + first, 1 - first)
        late_op = jnp.where(on_end, 1 - first, 2 + first)
        op = jnp.where(
            at == 0, first, jnp.where(at == 1, early, jnp.where(at == 2, late_op, 3 - first))
        )

        @pl.when(op == 0)
        def _():
            prepare(0)

        @pl.when(op == 1)
        def _():
            prepare(1)

        @pl.when(at == 0)
        def _():
            settle_facts()

        @pl.when(op == 2)
        def _():
            chain(0)

        @pl.when(op == 3)
        def _():
            chain(1)

        return carry

    lax.fori_loop(0, 4, slot, 0)

    for copy in fact_copies() + start_copies():
        copy.wait_send()

    @pl.when(below)
    def _():
        next_copy().wait_send()

    def settle(piece, carry):
        for copy in fix_copies(piece):
            copy.wait_send()
        for sweep in range(2):
            written(sweep, piece).wait()

            @pl.when(jnp.logical_not(is_last[sweep]))
            def _():
                for copy in wave_copies(sweep, piece):
                    copy.wait_send()

        return carry

    lax.fori_loop(0, pieces, settle, 0)


def per_device(
    source,
    cotangent,
    flux,
    pore_mask,
    upwind,
    side_link,
    local_inverse,
    flow_lift,
    side_lift,
    flow_trace,
    side_trace,
):
    levels, nodes, elems = source.shape
    tiles = elems // TILE
    pieces = tiles // GROUP
    width = GROUP * TILE
    extended = width + TILE
    whole = pl.BlockSpec(memory_space=pltpu.VMEM)
    away = pl.BlockSpec(memory_space=pltpu.HBM)
    dma = pltpu.SemaphoreType.DMA
    return pl.pallas_call(
        kernel,
        out_shape=(
            jax.ShapeDtypeStruct(source.shape, F32),
            jax.ShapeDtypeStruct(source.shape, F32),
        ),
        in_specs=[away, away] + [whole] * 9,
        out_specs=(away, away),
        scratch_shapes=[
            pltpu.VMEM((2, levels, nodes, elems), F32),
            pltpu.VMEM((2, levels, pieces, BOTH, extended), F32),
            pltpu.VMEM((levels, pieces, 1, extended), F32),
            pltpu.VMEM((levels, tiles, 2 * TILE, TILE), BF16),
            pltpu.VMEM((pieces, 2 * TILE, TILE), BF16),
            pltpu.VMEM((pieces, width, TILE), BF16),
            pltpu.VMEM((2, levels, pieces, 3 * BOTH, width), BF16),
            pltpu.VMEM((pieces, BOTH, width), F32),
            pltpu.VMEM((2, pieces, BOTH, extended), F32),
            pltpu.VMEM((2, pieces, BOTH, extended), F32),
            pltpu.VMEM((2, pieces, NEAR + FACE, TILE), F32),
            pltpu.VMEM((2, pieces, NEAR, TILE), F32),
            pltpu.VMEM((2, pieces, NEAR, TILE), F32),
            pltpu.VMEM((2, pieces, FACE, TILE), F32),
            pltpu.VMEM((2, pieces, FACE, TILE), F32),
            pltpu.VMEM((pieces, FACE, TILE), F32),
            pltpu.VMEM((pieces, FACE, TILE), F32),
            pltpu.VMEM((pieces, FACE, TILE), F32),
            pltpu.VMEM((pieces, 8, TILE), F32),
            pltpu.VMEM((pieces, 8, TILE), F32),
            pltpu.VMEM((pieces, 8, TILE), F32),
            pltpu.VMEM((pieces, 8, TILE), F32),
            pltpu.VMEM((pieces, FACE, TILE), F32),
            pltpu.VMEM((pieces, FACE, TILE), F32),
            pltpu.VMEM((pieces, FACE, TILE), F32),
            pltpu.VMEM((nodes, BOTH), F32),
            pltpu.VMEM((nodes + BOTH, 3 * nodes), F32),
            pltpu.VMEM((2, nodes + BOTH, 3 * nodes), BF16),
            pltpu.VMEM((2, BOTH, 3 * BOTH), BF16),
            pltpu.VMEM((2, nodes, 3 * BOTH), BF16),
            dma((2,)),
            dma((2, pieces)),
            dma((2, 2, pieces)),
            dma((4, 2, pieces)),
            dma((4, 2, pieces)),
            dma((4, pieces)),
            dma((4,)),
            dma((2,)),
            dma((4,)),
        ],
        compiler_params=pltpu.CompilerParams(
            collective_id=0, has_side_effects=True, vmem_limit_bytes=40 << 20
        ),
    )(
        source,
        cotangent,
        flux,
        pore_mask,
        upwind,
        side_link,
        local_inverse,
        flow_lift,
        side_lift,
        flow_trace,
        side_trace,
    )


def solution(mesh):
    placed = (
        P("flow", None, "cross"),
        P("flow", None, "cross"),
        P("flow", "cross"),
        P("flow", "cross"),
        P("flow", "cross"),
        P("flow", "cross"),
        P(),
        P(),
        P(),
        P(),
        P(),
    )
    return jax.shard_map(
        per_device,
        mesh=mesh,
        in_specs=placed,
        out_specs=(P("flow", None, "cross"), P("flow", None, "cross")),
        check_vma=False,
    )
```

time: 710 us -> 73.3 us (0.10)
  the two profiles are of different devices: /device:TPU:15 before, /device:TPU:32 now
where the time goes in v1:
time: 73.3 us; the launch traced here: 72.8 us
  Pallas kernels  64 us (87%)
  local copies, waits for them, and re-layouts  8.1 us (11%)
    pallas_call x1, Pallas kernels, per_device(): pl.pallas_call(kernel, out_shape=(jax.ShapeDtypeStruct(source.shape, F32)...  64 us
    unnamed x22, local copies, waits for them, and re-layouts  8.1 us

profile of v1, /device:TPU:32, one launch (start us, length us, event | category | flops | bytes accessed | tf_op | source)
XLA Modules:
  0.0 72.8 jit_solution(4316869577036331217)
XLA Ops:
  0.6 0.0 copy-start.2
  0.6 0.0 copy-start.5
  0.7 0.8 %copy.13.flow_lift = f32[64,16]{1,0:T(8,128)S(1)} copy(f32[64,16]{0,1:T(8,128)} %param.18) | data formatting | bytes 8192 | tf_op args[7]
  1.4 0.0 copy-start.3
  1.4 0.0 copy-start.4
  1.5 0.8 %copy.14.side_lift = f32[64,16]{1,0:T(8,128)S(1)} copy(f32[64,16]{0,1:T(8,128)} %param.19) | data formatting | bytes 8192 | tf_op args[8]
  2.3 0.0 copy-done.2
  2.3 0.0 copy-done.5
  2.3 0.0 copy-done.3
  2.3 0.0 copy-done.4
  2.3 0.0 copy-start
  2.3 1.2 %copy-done = f32[2,64,2048]{2,1,0:T(8,128)S(1)} copy-done((f32[2,64,2048]{2,1,0:T(8,128)S(1)}, f32[2,64,2048]{2,1,0:T(8,128)}, u32[]{:S(2)}) %copy-start) | copy-done | bytes 1048600
  3.5 0.0 copy-start.1
  3.5 1.2 %copy-done.1 = f32[2,64,2048]{2,1,0:T(8,128)S(1)} copy-done((f32[2,64,2048]{2,1,0:T(8,128)S(1)}, f32[2,64,2048]{2,1,0:T(8,128)}, u32[]{:S(2)}) %copy-start.1) | copy-done | bytes 1048600
  4.7 0.0 copy-start.6
  4.7 0.7 copy-done.6
  5.5 0.0 copy-start.7
  5.5 0.7 copy-done.7
  6.2 0.0 copy-start.8
  6.2 0.7 copy-done.8
  6.8 64.0 %shard_map.122 = (f32[2,64,2048]{2,1,0:T(8,128)S(1)}, f32[2,64,2048]{2,1,0:T(8,128)S(1)}) custom-call(f32[2,64,2048]{2,1,0:T(8,128)S(1)} %copy-done, f32[2,64,2048]{2,1,0:T(8,128)S(1)} %copy-done.1, f32[2,2048]{1,0:T(2,128)S(1)} %copy-done.3, s32[2,2048]{1,0:T(2,128)S(1)} %copy-done.4, s32[2,2048]{1,0:T(2,128)S(1)} %copy-done.5, s32[2,2048]{1,0:T(2,128)S(1)} %copy-done.6, ...), custom_call_target="tpu_custom_call" | custom-call | tf_op jit(solution)/shard_map/pallas_call | solution.py:666
  70.9 1.0 %copy.17 = f32[2,64,2048]{2,1,0:T(8,128)} copy(f32[2,64,2048]{2,1,0:T(8,128)S(1)} %get-tuple-element.4) | data formatting | bytes 2097152
  71.8 1.0 %copy.18 = f32[2,64,2048]{2,1,0:T(8,128)} copy(f32[2,64,2048]{2,1,0:T(8,128)S(1)} %get-tuple-element.5) | data formatting | bytes 2097152
Async XLA Ops:
  0.6 1.6 %copy-start.2 = (f32[64,64]{1,0:T(8,128)S(1)}, f32[64,64]{1,0:T(8,128)}, u32[]{:S(2)}) copy-start(f32[64,64]{1,0:T(8,128)} %local_inverse.1) | copy-start | bytes 49156
  0.6 1.6 %copy-start.5 = (s32[2,2048]{1,0:T(2,128)S(1)}, s32[2,2048]{1,0:T(2,128)}, u32[]{:S(2)}) copy-start(s32[2,2048]{1,0:T(2,128)} %upwind.1) | copy-start | bytes 49156
  1.4 0.8 %copy-start.3 = (f32[2,2048]{1,0:T(2,128)S(1)}, f32[2,2048]{1,0:T(2,128)}, u32[]{:S(2)}) copy-start(f32[2,2048]{1,0:T(2,128)} %flux.1) | copy-start | bytes 49156
  1.4 0.8 %copy-start.4 = (s32[2,2048]{1,0:T(2,128)S(1)}, s32[2,2048]{1,0:T(2,128)}, u32[]{:S(2)}) copy-start(s32[2,2048]{1,0:T(2,128)} %pore_mask.1) | copy-start | bytes 49156
  2.3 1.2 %copy-start = (f32[2,64,2048]{2,1,0:T(8,128)S(1)}, f32[2,64,2048]{2,1,0:T(8,128)}, u32[]{:S(2)}) copy-start(f32[2,64,2048]{2,1,0:T(8,128)} %source.1) | copy-start | bytes 3145732
  3.5 1.2 %copy-start.1 = (f32[2,64,2048]{2,1,0:T(8,128)S(1)}, f32[2,64,2048]{2,1,0:T(8,128)}, u32[]{:S(2)}) copy-start(f32[2,64,2048]{2,1,0:T(8,128)} %cotangent.1) | copy-start | bytes 3145732
  4.7 0.7 copy-start.6
  5.5 0.7 copy-start.7
  6.2 0.7 copy-start.8

commit v2 on v1

--- a/solution.py
+++ b/solution.py
@@ -13,6 +13,7 @@
 HALF = TILE // 2
 BOTH = 2 * FACE
 NEAR = 3 * FACE
+LIMIT = 60
 
 HIGH = lax.Precision.HIGHEST
 F32 = jnp.float32
@@ -51,13 +52,13 @@
 def kernel(
     source,
     cotangent,
-    flux,
-    pore_mask,
-    upwind,
-    side_link,
-    local_inverse,
-    flow_lift,
-    side_lift,
+    flux_away,
+    pore_mask_away,
+    upwind_away,
+    side_link_away,
+    local_inverse_away,
+    flow_lift_rows,
+    side_lift_rows,
     flow_trace,
     side_trace,
     concentration,
@@ -87,11 +88,18 @@
     start_out,
     start_left,
     start_right,
-    lift,
+    flux,
+    pore_mask,
+    upwind,
+    side_link,
+    local_inverse,
+    lift_rows,
+    trace_rows,
     wide,
     local_weight,
     chain_weight,
     out_weight,
+    small_sem,
     field_sem,
     done_sem,
     main_sem,
@@ -117,21 +125,47 @@
     downstream = (place + 1, place - 1)
     below, above = place > 0, place < flow_count - 1
 
-    def beside(steps):
-        return lax.rem(block + cross_count + steps, cross_count)
+    def inside(steps):
+        return (block + steps >= 0) & (block + steps < cross_count)
 
     def loaded(sweep):
         return pltpu.make_async_copy(inputs[sweep], field.at[sweep], field_sem.at[sweep])
 
-    loaded(0).start()
-    loaded(1).start()
+    small = (
+        (side_link_away, side_link),
+        (upwind_away, upwind),
+        (flux_away, flux),
+        (pore_mask_away, pore_mask),
+        (local_inverse_away, local_inverse),
+        (flow_trace, trace_rows.at[pl.ds(0, FACE)]),
+        (side_trace, trace_rows.at[pl.ds(FACE, FACE)]),
+        (flow_lift_rows, lift_rows.at[pl.ds(0, FACE)]),
+        (side_lift_rows, lift_rows.at[pl.ds(FACE, FACE)]),
+    )
+    fetches = [
+        pltpu.make_async_copy(src, dst, small_sem.at[n]) for n, (src, dst) in enumerate(small)
+    ]
+    for fetch in fetches:
+        fetch.start()
+
+    @pl.when(above)
+    def _():
+        loaded(0).start()
+        loaded(1).start()
+
+    @pl.when(jnp.logical_not(above))
+    def _():
+        loaded(1).start()
+        loaded(0).start()
 
     barrier = pltpu.get_barrier_semaphore()
 
     def greet(flow_at, steps):
-        pl.semaphore_signal(
-            barrier, inc=1, device_id=(flow_at, beside(steps)), device_id_type=MESH
-        )
+        @pl.when(inside(steps))
+        def _():
+            pl.semaphore_signal(
+                barrier, inc=1, device_id=(flow_at, block + steps), device_id_type=MESH
+            )
 
     greet(place, -1)
     greet(place, 1)
@@ -146,15 +180,20 @@
         for steps in range(-2, 3):
             greet(place + 1, steps)
 
+    in_line = [inside(steps).astype(jnp.int32) for steps in range(-2, 3)]
+    met = (below.astype(jnp.int32) + above.astype(jnp.int32)) * sum(in_line)
+    met = met + in_line[1] + in_line[3]
+
+    for fetch in fetches:
+        fetch.wait()
+
     inverse = local_inverse[...]
-    lift[:, 0:FACE] = flow_lift[...]
-    lift[:, FACE:BOTH] = side_lift[...]
-    lifts = lift[...]
-    trace = jnp.concatenate([flow_trace[...], side_trace[...]], axis=0)
+    lifts = lift_rows[...].T
+    trace = trace_rows[...]
     traced_inverse = jnp.dot(trace, inverse, precision=HIGH, preferred_element_type=F32)
     traced_lift = jnp.dot(trace, lifts, precision=HIGH, preferred_element_type=F32)
     widened(jnp.concatenate([inverse, traced_inverse], axis=0), wide, local_weight.at[0])
-    widened(jnp.concatenate([inverse.T, lifts.T], axis=0), wide, local_weight.at[1])
+    widened(jnp.concatenate([inverse.T, lift_rows[...]], axis=0), wide, local_weight.at[1])
     widened(traced_lift, wide, chain_weight.at[0])
     widened(traced_lift.T, wide, chain_weight.at[1])
     widened(lifts, wide, out_weight.at[0])
@@ -227,14 +266,15 @@
     lax.fori_loop(0, pieces, gather_facts, 0)
 
     def send(src, dst, send_sem, recv_sem, flow_at, steps):
-        return pltpu.make_async_remote_copy(
+        copy = pltpu.make_async_remote_copy(
             src_ref=src,
             dst_ref=dst,
             send_sem=send_sem,
             recv_sem=recv_sem,
-            device_id=(flow_at, beside(steps)),
+            device_id=(flow_at, block + steps),
             device_id_type=MESH,
         )
+        return copy, steps
 
     def pair(src, at_left, at_right, sem, flow_at, reach=1):
         return (
@@ -242,11 +282,27 @@
             send(src, at_right, sem(2), sem(3), flow_at, -reach),
         )
 
+    def each(copies, act, sign):
+        for copy, steps in copies:
+            if steps == 0:
+                act(copy)
+            else:
+                pl.when(inside(sign * steps))(lambda copy=copy: act(copy))
+
+    def start_all(copies):
+        each(copies, lambda copy: copy.start(), 1)
+
+    def wait_sent(copies):
+        each(copies, lambda copy: copy.wait_send(), 1)
+
+    def wait_received(copies):
+        each(copies, lambda copy: copy.wait_recv(), -1)
+
     def fact_copies():
         return pair(fact_out, fact_left, fact_right, lambda n: fact_sem.at[n], place)
 
-    def next_copy():
-        return send(fact_out, fact_next, next_sem.at[0], next_sem.at[1], place - 1, 0)
+    def next_copies():
+        return (send(fact_out, fact_next, next_sem.at[0], next_sem.at[1], place - 1, 0),)
 
     def start_copies():
         return pair(start_out, start_left, start_right, lambda n: start_sem.at[n], place)
@@ -287,14 +343,13 @@
         )
         return near + far + (main,)
 
-    pl.semaphore_wait(barrier, 2 + 5 * below.astype(jnp.int32) + 5 * above.astype(jnp.int32))
-
-    for copy in fact_copies():
-        copy.start()
+    pl.semaphore_wait(barrier, met)
+
+    start_all(fact_copies())
 
     @pl.when(below)
     def _():
-        next_copy().start()
+        start_all(next_copies())
 
     def one_hot(row, depth):
         rows = lax.broadcasted_iota(jnp.int32, (depth, TILE), 0)
@@ -319,12 +374,11 @@
     lax.fori_loop(0, pieces, build_pick, 0)
 
     def settle_facts():
-        for copy in fact_copies():
-            copy.wait_recv()
+        wait_received(fact_copies())
 
         @pl.when(above)
         def _():
-            next_copy().wait_recv()
+            wait_received(next_copies())
 
         @pl.when(jnp.logical_not(above))
         def _():
@@ -381,8 +435,7 @@
 
         lax.fori_loop(0, pieces, first_level, 0)
         if sweep == 0:
-            for copy in start_copies():
-                copy.start()
+            start_all(start_copies())
         lax.fori_loop(0, pieces, second_level, 0)
 
     def arrive(sweep, piece):
@@ -396,12 +449,10 @@
 
         @pl.when(jnp.logical_not(is_first[sweep]))
         def _():
-            for copy in wave_copies(sweep, piece):
-                copy.wait_recv()
+            wait_received(wave_copies(sweep, piece))
 
     def leave(sweep, piece):
-        for copy in wave_copies(sweep, piece):
-            copy.start()
+        start_all(wave_copies(sweep, piece))
 
     def picked(near, beyond, one_hots):
         near_high, near_low = near
@@ -507,8 +558,7 @@
         )
         own, edge = scattered(value[FACE:], 1, piece)
         fix_out[piece] = edge
-        for copy in fix_copies(piece):
-            copy.start()
+        start_all(fix_copies(piece))
         inbound = jnp.concatenate(
             [
                 jnp.concatenate([value[:FACE], none], axis=1),
@@ -543,8 +593,7 @@
         cols = columns_of(piece)
         for level in range(LEVELS_HERE):
             if sweep == 1 and level == 0:
-                for copy in fix_copies(piece):
-                    copy.wait_recv()
+                wait_received(fix_copies(piece))
                 edges = homeward(fix_left[piece], fix_right[piece])
                 sides = [
                     cut(late[piece, FACE:BOTH], at) + unpacked(edges, at) for at in range(GROUP)
@@ -563,8 +612,7 @@
     def chain(sweep):
         step = forward if sweep == 0 else adjoint
         if sweep == 0:
-            for copy in start_copies():
-                copy.wait_recv()
+            wait_received(start_copies())
 
             def begin(piece, carry):
                 lead[0, 0, piece, FACE:BOTH, width:whole_width] = inward(
@@ -619,23 +667,20 @@
 
     lax.fori_loop(0, 4, slot, 0)
 
-    for copy in fact_copies() + start_copies():
-        copy.wait_send()
+    wait_sent(fact_copies() + start_copies())
 
     @pl.when(below)
     def _():
-        next_copy().wait_send()
+        wait_sent(next_copies())
 
     def settle(piece, carry):
-        for copy in fix_copies(piece):
-            copy.wait_send()
+        wait_sent(fix_copies(piece))
         for sweep in range(2):
             written(sweep, piece).wait()
 
             @pl.when(jnp.logical_not(is_last[sweep]))
             def _():
-                for copy in wave_copies(sweep, piece):
-                    copy.wait_send()
+                wait_sent(wave_copies(sweep, piece))
 
         return carry
 
@@ -660,7 +705,6 @@
     pieces = tiles // GROUP
     width = GROUP * TILE
     extended = width + TILE
-    whole = pl.BlockSpec(memory_space=pltpu.VMEM)
     away = pl.BlockSpec(memory_space=pltpu.HBM)
     dma = pltpu.SemaphoreType.DMA
     return pl.pallas_call(
@@ -669,7 +713,7 @@
             jax.ShapeDtypeStruct(source.shape, F32),
             jax.ShapeDtypeStruct(source.shape, F32),
         ),
-        in_specs=[away, away] + [whole] * 9,
+        in_specs=[away] * 11,
         out_specs=(away, away),
         scratch_shapes=[
             pltpu.VMEM((2, levels, nodes, elems), F32),
@@ -697,11 +741,18 @@
             pltpu.VMEM((pieces, FACE, TILE), F32),
             pltpu.VMEM((pieces, FACE, TILE), F32),
             pltpu.VMEM((pieces, FACE, TILE), F32),
-            pltpu.VMEM((nodes, BOTH), F32),
+            pltpu.VMEM((levels, elems), F32),
+            pltpu.VMEM((levels, elems), jnp.int32),
+            pltpu.VMEM((levels, elems), jnp.int32),
+            pltpu.VMEM((levels, elems), jnp.int32),
+            pltpu.VMEM((nodes, nodes), F32),
+            pltpu.VMEM((BOTH, nodes), F32),
+            pltpu.VMEM((BOTH, nodes), F32),
             pltpu.VMEM((nodes + BOTH, 3 * nodes), F32),
             pltpu.VMEM((2, nodes + BOTH, 3 * nodes), BF16),
             pltpu.VMEM((2, BOTH, 3 * BOTH), BF16),
             pltpu.VMEM((2, nodes, 3 * BOTH), BF16),
+            dma((9,)),
             dma((2,)),
             dma((2, pieces)),
             dma((2, 2, pieces)),
@@ -713,7 +764,7 @@
             dma((4,)),
         ],
         compiler_params=pltpu.CompilerParams(
-            collective_id=0, has_side_effects=True, vmem_limit_bytes=40 << 20
+            collective_id=0, has_side_effects=True, vmem_limit_bytes=LIMIT << 20
         ),
     )(
         source,
@@ -723,8 +774,8 @@
         upwind,
         side_link,
         local_inverse,
-        flow_lift,
-        side_lift,
+        flow_lift.T,
+        side_lift.T,
         flow_trace,
         side_trace,
     )

time: 73.3 us -> 65.7 us (0.90)
  the two profiles are of different devices: /device:TPU:32 before, /device:TPU:6 now
where the time goes in v2:
time: 65.7 us; the launch traced here: 65.4 us
  Pallas kernels  61.4 us (93%)
  local copies, waits for them, and re-layouts  3.36 us (5%)
    pallas_call x1, Pallas kernels, per_device(): pl.pallas_call(kernel, out_shape=(jax.ShapeDtypeStruct(source.shape, F32)...  61.4 us
    unnamed x4, local copies, waits for them, and re-layouts  3.36 us

profile of v2, /device:TPU:6, one launch (start us, length us, event | category | flops | bytes accessed | tf_op | source)
XLA Modules:
  0.0 65.4 jit_solution(11685661139409870945)
XLA Ops:
  0.6 61.4 %shard_map.122 = (f32[2,64,2048]{2,1,0:T(8,128)}, f32[2,64,2048]{2,1,0:T(8,128)}) custom-call(f32[2,64,2048]{2,1,0:T(8,128)} %source.1, f32[2,64,2048]{2,1,0:T(8,128)} %cotangent.1, f32[2,2048]{1,0:T(2,128)} %flux_away.1, s32[2,2048]{1,0:T(2,128)} %pore_mask_away.1, s32[2,2048]{1,0:T(2,128)} %upwind_away.1, s32[2,2048]{1,0:T(2,128)} %side_link_away.1, ...), custom_call_target="tpu_custom_call" | custom-call | tf_op jit(solution)/shard_map/pallas_call | solution.py:710
  62.1 0.0 copy-start
  62.1 2.4 %copy.15 = f32[2,64,2048]{2,1,0:T(8,128)} copy(f32[2,64,2048]{2,1,0:T(8,128)} %get-tuple-element.4) | data formatting | bytes 2097152
  64.4 0.0 copy-done
  64.4 1.0 %copy.16 = f32[2,64,2048]{2,1,0:T(8,128)} copy(f32[2,64,2048]{2,1,0:T(8,128)S(1)} %copy-done) | data formatting | bytes 2097152
Async XLA Ops:
  62.1 2.4 %copy-start = (f32[2,64,2048]{2,1,0:T(8,128)S(1)}, f32[2,64,2048]{2,1,0:T(8,128)}, u32[]{:S(2)}) copy-start(f32[2,64,2048]{2,1,0:T(8,128)} %get-tuple-element.5) | copy-start | bytes 3145732

commit v3 on v2

--- a/solution.py
+++ b/solution.py
@@ -12,8 +12,8 @@
 GROUP = 4
 HALF = TILE // 2
 BOTH = 2 * FACE
-NEAR = 3 * FACE
-LIMIT = 60
+NEAR = 2 * FACE
+LIMIT = 48
 
 HIGH = lax.Precision.HIGHEST
 F32 = jnp.float32
@@ -63,7 +63,6 @@
     side_trace,
     concentration,
     sensitivity,
-    field,
     lead,
     scale,
     pick,
@@ -101,7 +100,6 @@
     out_weight,
     small_sem,
     field_sem,
-    done_sem,
     main_sem,
     near_sem,
     far_sem,
@@ -115,9 +113,9 @@
     place = lax.axis_index("flow")
     block = lax.axis_index("cross")
     pieces = main_in.shape[1]
-    whole_width = main_in.shape[3]
-    width = whole_width - TILE
-    nodes = field.shape[2]
+    width = main_in.shape[3]
+    whole_width = width + TILE
+    nodes = concentration.shape[1]
     inputs = (source, cotangent)
     results = (concentration, sensitivity)
     is_first = (place == 0, place == flow_count - 1)
@@ -129,7 +127,7 @@
         return (block + steps >= 0) & (block + steps < cross_count)
 
     def loaded(sweep):
-        return pltpu.make_async_copy(inputs[sweep], field.at[sweep], field_sem.at[sweep])
+        return pltpu.make_async_copy(inputs[sweep], results[sweep], field_sem.at[sweep])
 
     small = (
         (side_link_away, side_link),
@@ -237,6 +235,20 @@
         opened = jnp.where(lane < HALF, *is_open(reach)[::-1])
         return jnp.where(opened > 0, jnp.where(lane < HALF, from_right, from_left), 0.0)
 
+    def swapped(value):
+        return pltpu.roll(value, HALF, 1)
+
+    def folded(first, second, third):
+        lane = lanes(FACE)
+        low = jnp.where(lane < HALF, first, swapped(second))
+        high = jnp.where(lane < HALF, swapped(first), second)
+        return jnp.concatenate([low, third, high], axis=0)
+
+    def unfolded(lows, highs):
+        low = jnp.concatenate([lows[:FACE], swapped(lows[:FACE]), lows[FACE:]], axis=0)
+        high = jnp.concatenate([swapped(highs[FACE:]), highs[FACE:], highs[:FACE]], axis=0)
+        return low, high
+
     def columns_of(piece):
         return pl.ds(pl.multiple_of(piece * width, width), width)
 
@@ -326,15 +338,29 @@
             flow_at,
             0,
         )
-        near = pair(
-            near_out.at[sweep, piece, pl.ds(0, NEAR)],
-            near_left.at[sweep, piece],
-            near_right.at[sweep, piece],
-            lambda n: near_sem.at[n, sweep, piece],
-            flow_at,
+        low = near_out.at[sweep, piece, pl.ds(0, NEAR)]
+        high = near_out.at[sweep, piece, pl.ds(FACE, NEAR)]
+        ahead, back = (low, high) if sweep == 0 else (high, low)
+        near = (
+            send(
+                ahead,
+                near_left.at[sweep, piece],
+                near_sem.at[0, sweep, piece],
+                near_sem.at[1, sweep, piece],
+                flow_at,
+                1,
+            ),
+            send(
+                back,
+                near_right.at[sweep, piece],
+                near_sem.at[2, sweep, piece],
+                near_sem.at[3, sweep, piece],
+                flow_at,
+                -1,
+            ),
         )
         far = pair(
-            near_out.at[sweep, piece, pl.ds(NEAR, FACE)],
+            near_out.at[sweep, piece, pl.ds(FACE if sweep == 0 else 3 * FACE, FACE)],
             far_left.at[sweep, piece],
             far_right.at[sweep, piece],
             lambda n: far_sem.at[n, sweep, piece],
@@ -415,9 +441,9 @@
 
         def one(level, piece):
             cols = columns_of(piece)
-            value = product(local_weight[sweep], stacked(field[sweep, level, :, cols]))
+            value = product(local_weight[sweep], stacked(results[sweep][level, :, cols]))
             mask = live(level, piece)
-            field[sweep, level, :, cols] = mask * value[:nodes]
+            results[sweep][level, :, cols] = mask * value[:nodes]
             added = (mask if sweep == 0 else scale[level, piece, :, 0:width]) * value[nodes:]
             lead[sweep, level, piece, :, 0:width] = added
             if level == 0:
@@ -441,7 +467,7 @@
     def arrive(sweep, piece):
         @pl.when(is_first[sweep])
         def _():
-            main_in[sweep, piece] = jnp.zeros((BOTH, whole_width), F32)
+            main_in[sweep, piece] = jnp.zeros((BOTH, width), F32)
             near_left[sweep, piece] = jnp.zeros((NEAR, TILE), F32)
             near_right[sweep, piece] = jnp.zeros((NEAR, TILE), F32)
             far_left[sweep, piece] = jnp.zeros((FACE, TILE), F32)
@@ -494,16 +520,16 @@
     def forward(piece):
         arrive(0, piece)
         main = main_in[0, piece]
-        near = inward(near_left[0, piece], near_right[0, piece])
+        near = inward(*unfolded(near_left[0, piece], near_right[0, piece]))
         outer = inward(far_left[0, piece], far_right[0, piece], 2)
-        sides = gathered(main[FACE:, :width], near[BOTH:], 0, piece)
+        sides = gathered(main[FACE:], near[BOTH:], 0, piece)
         sides.append(
             near[FACE:BOTH]
-            + picked(halves(main[FACE:, width:]), halves(outer), pick_beside[piece])
+            + picked(halves(packed(main[FACE:])), halves(outer), pick_beside[piece])
         )
         inbound = jnp.concatenate(
             [
-                jnp.concatenate([main[:FACE, :width], near[:FACE]], axis=1),
+                jnp.concatenate([main[:FACE], near[:FACE]], axis=1),
                 jnp.concatenate(sides, axis=1),
             ],
             axis=0,
@@ -524,21 +550,20 @@
             )
             edges = packed(value)
             ahead = product(jnp.concatenate(halves(value[FACE:]), axis=0), pick_next[piece])
-            main_out[0, piece, :, 0:width] = value
-            main_out[0, piece, :, width:whole_width] = edges
-            near_out[0, piece, 0:FACE] = edges[:FACE]
-            near_out[0, piece, FACE:BOTH] = ahead[:FACE] + ahead[FACE:]
-            near_out[0, piece, BOTH:NEAR] = edges[FACE:]
-            near_out[0, piece, NEAR : NEAR + FACE] = edges[FACE:]
+            main_out[0, piece] = value
+            near_out[0, piece, 0 : 3 * FACE] = folded(
+                edges[:FACE], ahead[:FACE] + ahead[FACE:], edges[FACE:]
+            )
             leave(0, piece)
 
     def adjoint(piece):
         arrive(1, piece)
         main = main_in[1, piece]
-        near = homeward(near_left[1, piece], near_right[1, piece])
+        highs, lows = near_left[1, piece], near_right[1, piece]
+        near = homeward(*unfolded(lows, highs)[::-1])
         outer = homeward(far_left[1, piece], far_right[1, piece], 2)
         edges = jnp.concatenate(
-            [near[:FACE], main[FACE:, width:] + near[BOTH:] + outer], axis=0
+            [near[:FACE], near[BOTH:] + outer], axis=0
         )
         behind = spread(near[FACE:BOTH], pick_next[piece])
         none = jnp.zeros((FACE, TILE), F32)
@@ -575,19 +600,14 @@
             )
             own, edge = scattered(value[FACE:, :width], 0, piece)
             around = spread(value[FACE:, width:], pick_beside[piece])
-            own.append(around[:, :TILE])
-            main_out[1, piece, 0:FACE] = jnp.concatenate([value[:FACE, :width], none], axis=1)
+            own = [own[at] + unpacked(around[:, :TILE], at) for at in range(GROUP)]
+            main_out[1, piece, 0:FACE] = value[:FACE, :width]
             main_out[1, piece, FACE:BOTH] = jnp.concatenate(own, axis=1)
-            near_out[1, piece, 0:BOTH] = value[:, width:]
-            near_out[1, piece, BOTH:NEAR] = edge
-            near_out[1, piece, NEAR : NEAR + FACE] = around[:, TILE:]
+            near_out[1, piece, 0 : 3 * FACE] = folded(
+                value[:FACE, width:], value[FACE:, width:], edge
+            )
+            near_out[1, piece, 3 * FACE : 4 * FACE] = around[:, TILE:]
             leave(1, piece)
-
-    def written(sweep, piece):
-        cols = columns_of(piece)
-        return pltpu.make_async_copy(
-            field.at[sweep, :, :, cols], results[sweep].at[:, :, cols], done_sem.at[sweep, piece]
-        )
 
     def finish(sweep, piece):
         cols = columns_of(piece)
@@ -606,8 +626,7 @@
             else:
                 operand = kept[sweep, level, piece]
             factor = scale[level, piece, :, 0:width] if sweep == 0 else live(level, piece)
-            field[sweep, level, :, cols] += factor * product(out_weight[sweep], operand)
-        written(sweep, piece).start()
+            results[sweep][level, :, cols] += factor * product(out_weight[sweep], operand)
 
     def chain(sweep):
         step = forward if sweep == 0 else adjoint
@@ -676,8 +695,6 @@
     def settle(piece, carry):
         wait_sent(fix_copies(piece))
         for sweep in range(2):
-            written(sweep, piece).wait()
-
             @pl.when(jnp.logical_not(is_last[sweep]))
             def _():
                 wait_sent(wave_copies(sweep, piece))
@@ -706,17 +723,17 @@
     width = GROUP * TILE
     extended = width + TILE
     away = pl.BlockSpec(memory_space=pltpu.HBM)
+    here = pl.BlockSpec(memory_space=pltpu.VMEM)
     dma = pltpu.SemaphoreType.DMA
     return pl.pallas_call(
         kernel,
         out_shape=(
-            jax.ShapeDtypeStruct(source.shape, F32),
-            jax.ShapeDtypeStruct(source.shape, F32),
+            pltpu.VMEM(source.shape, F32),
+            pltpu.VMEM(source.shape, F32),
         ),
         in_specs=[away] * 11,
-        out_specs=(away, away),
+        out_specs=(here, here),
         scratch_shapes=[
-            pltpu.VMEM((2, levels, nodes, elems), F32),
             pltpu.VMEM((2, levels, pieces, BOTH, extended), F32),
             pltpu.VMEM((levels, pieces, 1, extended), F32),
             pltpu.VMEM((levels, tiles, 2 * TILE, TILE), BF16),
@@ -724,9 +741,9 @@
             pltpu.VMEM((pieces, width, TILE), BF16),
             pltpu.VMEM((2, levels, pieces, 3 * BOTH, width), BF16),
             pltpu.VMEM((pieces, BOTH, width), F32),
-            pltpu.VMEM((2, pieces, BOTH, extended), F32),
-            pltpu.VMEM((2, pieces, BOTH, extended), F32),
-            pltpu.VMEM((2, pieces, NEAR + FACE, TILE), F32),
+            pltpu.VMEM((2, pieces, BOTH, width), F32),
+            pltpu.VMEM((2, pieces, BOTH, width), F32),
+            pltpu.VMEM((2, pieces, 4 * FACE, TILE), F32),
             pltpu.VMEM((2, pieces, NEAR, TILE), F32),
             pltpu.VMEM((2, pieces, NEAR, TILE), F32),
             pltpu.VMEM((2, pieces, FACE, TILE), F32),
@@ -754,7 +771,6 @@
             pltpu.VMEM((2, nodes, 3 * BOTH), BF16),
             dma((9,)),
             dma((2,)),
-            dma((2, pieces)),
             dma((2, 2, pieces)),
             dma((4, 2, pieces)),
             dma((4, 2, pieces)),
@@ -767,17 +783,22 @@
             collective_id=0, has_side_effects=True, vmem_limit_bytes=LIMIT << 20
         ),
     )(
-        source,
-        cotangent,
-        flux,
-        pore_mask,
-        upwind,
-        side_link,
-        local_inverse,
-        flow_lift.T,
-        side_lift.T,
-        flow_trace,
-        side_trace,
+        *(
+            pltpu.with_memory_space_constraint(operand, pltpu.HBM)
+            for operand in (
+                source,
+                cotangent,
+                flux,
+                pore_mask,
+                upwind,
+                side_link,
+                local_inverse,
+                flow_lift.T,
+                side_lift.T,
+                flow_trace,
+                side_trace,
+            )
+        )
     )
 
 

time: 65.7 us -> 61.8 us (0.941)
  Pallas kernels: 61.4 us -> 59.1 us
  local copies, waits for them, and re-layouts: 3.36 us -> 1.94 us
    pallas_call x1, Pallas kernels: 61.4 us -> 59.1 us  [per_device(): pl.pallas_call(kernel, out_shape=(pltpu.VMEM(source.shape, F32), pltpu.VM...]
    unnamed x4 -> x2, local copies, waits for them, and re-layouts: 3.36 us -> 1.94 us
where the time goes in v3:
time: 61.8 us; the launch traced here: 61.6 us
  Pallas kernels  59.1 us (96%)
  local copies, waits for them, and re-layouts  1.94 us (3%)
  between operations  0.64 us (1%)
    pallas_call x1, Pallas kernels, per_device(): pl.pallas_call(kernel, out_shape=(pltpu.VMEM(source.shape, F32), pltpu.VM...  59.1 us
    unnamed x2, local copies, waits for them, and re-layouts  1.94 us

profile of v3, /device:TPU:6, one launch (start us, length us, event | category | flops | bytes accessed | tf_op | source)
XLA Modules:
  0.0 61.6 jit_solution(5970956348039006484)
XLA Ops:
  0.6 59.1 %shard_map.122 = (f32[2,64,2048]{2,1,0:T(8,128)S(1)}, f32[2,64,2048]{2,1,0:T(8,128)S(1)}) custom-call(f32[2,64,2048]{2,1,0:T(8,128)} %source.1, f32[2,64,2048]{2,1,0:T(8,128)} %cotangent.1, f32[2,2048]{1,0:T(2,128)} %flux_away.1, s32[2,2048]{1,0:T(2,128)} %pore_mask_away.1, s32[2,2048]{1,0:T(2,128)} %upwind_away.1, s32[2,2048]{1,0:T(2,128)} %side_link_away.1, ...), custom_call_target="tpu_custom_call" | custom-call | tf_op jit(solution)/shard_map/pallas_call | solution.py:728
  59.7 1.0 %copy.15 = f32[2,64,2048]{2,1,0:T(8,128)} copy(f32[2,64,2048]{2,1,0:T(8,128)S(1)} %get-tuple-element.2) | data formatting | bytes 2097152
  60.7 1.0 %copy.16 = f32[2,64,2048]{2,1,0:T(8,128)} copy(f32[2,64,2048]{2,1,0:T(8,128)S(1)} %get-tuple-element.3) | data formatting | bytes 2097152

commit v4 on v3

--- a/solution.py
+++ b/solution.py
@@ -238,11 +238,11 @@
     def swapped(value):
         return pltpu.roll(value, HALF, 1)
 
-    def folded(first, second, third):
+    def folded(first, second):
         lane = lanes(FACE)
         low = jnp.where(lane < HALF, first, swapped(second))
         high = jnp.where(lane < HALF, swapped(first), second)
-        return jnp.concatenate([low, third, high], axis=0)
+        return low, high
 
     def unfolded(lows, highs):
         low = jnp.concatenate([lows[:FACE], swapped(lows[:FACE]), lows[FACE:]], axis=0)
@@ -367,7 +367,7 @@
             flow_at,
             2,
         )
-        return near + far + (main,)
+        return far + near + (main,)
 
     pl.semaphore_wait(barrier, met)
 
@@ -477,8 +477,11 @@
         def _():
             wait_received(wave_copies(sweep, piece))
 
+    def leave_far(sweep, piece):
+        start_all(wave_copies(sweep, piece)[:2])
+
     def leave(sweep, piece):
-        start_all(wave_copies(sweep, piece))
+        start_all(wave_copies(sweep, piece)[2:])
 
     def picked(near, beyond, one_hots):
         near_high, near_low = near
@@ -549,11 +552,13 @@
                 chain_weight[0], operand
             )
             edges = packed(value)
+            near_out[0, piece, FACE : 2 * FACE] = edges[FACE:]
+            leave_far(0, piece)
             ahead = product(jnp.concatenate(halves(value[FACE:]), axis=0), pick_next[piece])
             main_out[0, piece] = value
-            near_out[0, piece, 0 : 3 * FACE] = folded(
-                edges[:FACE], ahead[:FACE] + ahead[FACE:], edges[FACE:]
-            )
+            low, high = folded(edges[:FACE], ahead[:FACE] + ahead[FACE:])
+            near_out[0, piece, 0:FACE] = low
+            near_out[0, piece, 2 * FACE : 3 * FACE] = high
             leave(0, piece)
 
     def adjoint(piece):
@@ -583,7 +588,6 @@
         )
         own, edge = scattered(value[FACE:], 1, piece)
         fix_out[piece] = edge
-        start_all(fix_copies(piece))
         inbound = jnp.concatenate(
             [
                 jnp.concatenate([value[:FACE], none], axis=1),
@@ -598,35 +602,36 @@
             value = lead[1, 0, piece] + scale[0, piece] * product(
                 chain_weight[1], stacked(inbound)
             )
+            around = spread(value[FACE:, width:], pick_beside[piece])
+            near_out[1, piece, 3 * FACE : 4 * FACE] = around[:, TILE:]
+            leave_far(1, piece)
             own, edge = scattered(value[FACE:, :width], 0, piece)
-            around = spread(value[FACE:, width:], pick_beside[piece])
             own = [own[at] + unpacked(around[:, :TILE], at) for at in range(GROUP)]
             main_out[1, piece, 0:FACE] = value[:FACE, :width]
             main_out[1, piece, FACE:BOTH] = jnp.concatenate(own, axis=1)
-            near_out[1, piece, 0 : 3 * FACE] = folded(
-                value[:FACE, width:], value[FACE:, width:], edge
+            low, high = folded(value[:FACE, width:], value[FACE:, width:])
+            near_out[1, piece, 0:FACE] = low
+            near_out[1, piece, FACE : 2 * FACE] = edge
+            near_out[1, piece, 2 * FACE : 3 * FACE] = high
+            leave(1, piece)
+
+        start_all(fix_copies(piece))
+
+    def finish(sweep, level, piece):
+        cols = columns_of(piece)
+        if sweep == 1 and level == 0:
+            wait_received(fix_copies(piece))
+            edges = homeward(fix_left[piece], fix_right[piece])
+            sides = [
+                cut(late[piece, FACE:BOTH], at) + unpacked(edges, at) for at in range(GROUP)
+            ]
+            operand = stacked(
+                jnp.concatenate([late[piece, 0:FACE], jnp.concatenate(sides, axis=1)], axis=0)
             )
-            near_out[1, piece, 3 * FACE : 4 * FACE] = around[:, TILE:]
-            leave(1, piece)
-
-    def finish(sweep, piece):
-        cols = columns_of(piece)
-        for level in range(LEVELS_HERE):
-            if sweep == 1 and level == 0:
-                wait_received(fix_copies(piece))
-                edges = homeward(fix_left[piece], fix_right[piece])
-                sides = [
-                    cut(late[piece, FACE:BOTH], at) + unpacked(edges, at) for at in range(GROUP)
-                ]
-                operand = stacked(
-                    jnp.concatenate(
-                        [late[piece, 0:FACE], jnp.concatenate(sides, axis=1)], axis=0
-                    )
-                )
-            else:
-                operand = kept[sweep, level, piece]
-            factor = scale[level, piece, :, 0:width] if sweep == 0 else live(level, piece)
-            results[sweep][level, :, cols] += factor * product(out_weight[sweep], operand)
+        else:
+            operand = kept[sweep, level, piece]
+        factor = scale[level, piece, :, 0:width] if sweep == 0 else live(level, piece)
+        results[sweep][level, :, cols] += factor * product(out_weight[sweep], operand)
 
     def chain(sweep):
         step = forward if sweep == 0 else adjoint
@@ -645,11 +650,16 @@
             step(piece)
             return carry
 
+        def upper(piece, carry):
+            finish(sweep, 1, piece)
+            return carry
+
         def last(piece, carry):
-            finish(sweep, piece)
+            finish(sweep, 0, piece)
             return carry
 
         lax.fori_loop(0, pieces, one, 0)
+        lax.fori_loop(0, pieces, upper, 0)
         lax.fori_loop(0, pieces, last, 0)
 
     first = (place >= flow_count // 2).astype(jnp.int32)

time: 61.8 us -> 60.3 us (0.976)
  Pallas kernels: 59.1 us -> 57.5 us
    pallas_call x1, Pallas kernels: 59.1 us -> 57.5 us  [per_device(): pl.pallas_call(kernel, out_shape=(pltpu.VMEM(source.shape, F32), pltpu.VM...]
where the time goes in v4:
time: 60.3 us; the launch traced here: 60.1 us
  Pallas kernels  57.5 us (95%)
  local copies, waits for them, and re-layouts  1.94 us (3%)
  between operations  0.64 us (1%)
    pallas_call x1, Pallas kernels, per_device(): pl.pallas_call(kernel, out_shape=(pltpu.VMEM(source.shape, F32), pltpu.VM...  57.5 us
    unnamed x2, local copies, waits for them, and re-layouts  1.94 us

profile of v4, /device:TPU:6, one launch (start us, length us, event | category | flops | bytes accessed | tf_op | source)
XLA Modules:
  0.0 60.1 jit_solution(2921568698697808939)
XLA Ops:
  0.6 57.5 %shard_map.122 = (f32[2,64,2048]{2,1,0:T(8,128)S(1)}, f32[2,64,2048]{2,1,0:T(8,128)S(1)}) custom-call(f32[2,64,2048]{2,1,0:T(8,128)} %source.1, f32[2,64,2048]{2,1,0:T(8,128)} %cotangent.1, f32[2,2048]{1,0:T(2,128)} %flux_away.1, s32[2,2048]{1,0:T(2,128)} %pore_mask_away.1, s32[2,2048]{1,0:T(2,128)} %upwind_away.1, s32[2,2048]{1,0:T(2,128)} %side_link_away.1, ...), custom_call_target="tpu_custom_call" | custom-call | tf_op jit(solution)/shard_map/pallas_call | solution.py:738
  58.2 1.0 %copy.15 = f32[2,64,2048]{2,1,0:T(8,128)} copy(f32[2,64,2048]{2,1,0:T(8,128)S(1)} %get-tuple-element.2) | data formatting | bytes 2097152
  59.1 1.0 %copy.16 = f32[2,64,2048]{2,1,0:T(8,128)} copy(f32[2,64,2048]{2,1,0:T(8,128)S(1)} %get-tuple-element.3) | data formatting | bytes 2097152

commit v5 on v4

--- a/solution.py
+++ b/solution.py
@@ -182,20 +182,8 @@
     met = (below.astype(jnp.int32) + above.astype(jnp.int32)) * sum(in_line)
     met = met + in_line[1] + in_line[3]
 
-    for fetch in fetches:
+    for fetch in fetches[:4]:
         fetch.wait()
-
-    inverse = local_inverse[...]
-    lifts = lift_rows[...].T
-    trace = trace_rows[...]
-    traced_inverse = jnp.dot(trace, inverse, precision=HIGH, preferred_element_type=F32)
-    traced_lift = jnp.dot(trace, lifts, precision=HIGH, preferred_element_type=F32)
-    widened(jnp.concatenate([inverse, traced_inverse], axis=0), wide, local_weight.at[0])
-    widened(jnp.concatenate([inverse.T, lift_rows[...]], axis=0), wide, local_weight.at[1])
-    widened(traced_lift, wide, chain_weight.at[0])
-    widened(traced_lift.T, wide, chain_weight.at[1])
-    widened(lifts, wide, out_weight.at[0])
-    widened(traced_inverse.T, wide, out_weight.at[1])
 
     def lanes(rows):
         return lax.broadcasted_iota(jnp.int32, (rows, TILE), 1)
@@ -377,6 +365,21 @@
     def _():
         start_all(next_copies())
 
+    for fetch in fetches[4:]:
+        fetch.wait()
+
+    inverse = local_inverse[...]
+    lifts = lift_rows[...].T
+    trace = trace_rows[...]
+    traced_inverse = jnp.dot(trace, inverse, precision=HIGH, preferred_element_type=F32)
+    traced_lift = jnp.dot(trace, lifts, precision=HIGH, preferred_element_type=F32)
+    widened(jnp.concatenate([inverse, traced_inverse], axis=0), wide, local_weight.at[0])
+    widened(jnp.concatenate([inverse.T, lift_rows[...]], axis=0), wide, local_weight.at[1])
+    widened(traced_lift, wide, chain_weight.at[0])
+    widened(traced_lift.T, wide, chain_weight.at[1])
+    widened(lifts, wide, out_weight.at[0])
+    widened(traced_inverse.T, wide, out_weight.at[1])
+
     def one_hot(row, depth):
         rows = lax.broadcasted_iota(jnp.int32, (depth, TILE), 0)
         return jnp.where(rows == row, 1.0, 0.0).astype(BF16)
@@ -480,8 +483,11 @@
     def leave_far(sweep, piece):
         start_all(wave_copies(sweep, piece)[:2])
 
+    def leave_near(sweep, piece):
+        start_all(wave_copies(sweep, piece)[2:4])
+
     def leave(sweep, piece):
-        start_all(wave_copies(sweep, piece)[2:])
+        start_all(wave_copies(sweep, piece)[4:])
 
     def picked(near, beyond, one_hots):
         near_high, near_low = near
@@ -555,10 +561,11 @@
             near_out[0, piece, FACE : 2 * FACE] = edges[FACE:]
             leave_far(0, piece)
             ahead = product(jnp.concatenate(halves(value[FACE:]), axis=0), pick_next[piece])
-            main_out[0, piece] = value
             low, high = folded(edges[:FACE], ahead[:FACE] + ahead[FACE:])
             near_out[0, piece, 0:FACE] = low
             near_out[0, piece, 2 * FACE : 3 * FACE] = high
+            leave_near(0, piece)
+            main_out[0, piece] = value
             leave(0, piece)
 
     def adjoint(piece):
@@ -606,13 +613,14 @@
             near_out[1, piece, 3 * FACE : 4 * FACE] = around[:, TILE:]
             leave_far(1, piece)
             own, edge = scattered(value[FACE:, :width], 0, piece)
-            own = [own[at] + unpacked(around[:, :TILE], at) for at in range(GROUP)]
-            main_out[1, piece, 0:FACE] = value[:FACE, :width]
-            main_out[1, piece, FACE:BOTH] = jnp.concatenate(own, axis=1)
             low, high = folded(value[:FACE, width:], value[FACE:, width:])
             near_out[1, piece, 0:FACE] = low
             near_out[1, piece, FACE : 2 * FACE] = edge
             near_out[1, piece, 2 * FACE : 3 * FACE] = high
+            leave_near(1, piece)
+            own = [own[at] + unpacked(around[:, :TILE], at) for at in range(GROUP)]
+            main_out[1, piece, 0:FACE] = value[:FACE, :width]
+            main_out[1, piece, FACE:BOTH] = jnp.concatenate(own, axis=1)
             leave(1, piece)
 
         start_all(fix_copies(piece))

time: 60.3 us -> 60.8 us (level)
  no operation moved by 1% of the time
where the time goes in v5:
time: 60.8 us; the launch traced here: 60.6 us
  Pallas kernels  58 us (95%)
  local copies, waits for them, and re-layouts  1.94 us (3%)
  between operations  0.64 us (1%)
    pallas_call x1, Pallas kernels, per_device(): pl.pallas_call(kernel, out_shape=(pltpu.VMEM(source.shape, F32), pltpu.VM...  58 us
    unnamed x2, local copies, waits for them, and re-layouts  1.94 us

profile of v5, /device:TPU:6, one launch (start us, length us, event | category | flops | bytes accessed | tf_op | source)
XLA Modules:
  0.0 60.6 jit_solution(4071572181930372252)
XLA Ops:
  0.6 58.0 %shard_map.122 = (f32[2,64,2048]{2,1,0:T(8,128)S(1)}, f32[2,64,2048]{2,1,0:T(8,128)S(1)}) custom-call(f32[2,64,2048]{2,1,0:T(8,128)} %source.1, f32[2,64,2048]{2,1,0:T(8,128)} %cotangent.1, f32[2,2048]{1,0:T(2,128)} %flux_away.1, s32[2,2048]{1,0:T(2,128)} %pore_mask_away.1, s32[2,2048]{1,0:T(2,128)} %upwind_away.1, s32[2,2048]{1,0:T(2,128)} %side_link_away.1, ...), custom_call_target="tpu_custom_call" | custom-call | tf_op jit(solution)/shard_map/pallas_call | solution.py:746
  58.7 1.0 %copy.15 = f32[2,64,2048]{2,1,0:T(8,128)} copy(f32[2,64,2048]{2,1,0:T(8,128)S(1)} %get-tuple-element.2) | data formatting | bytes 2097152
  59.6 1.0 %copy.16 = f32[2,64,2048]{2,1,0:T(8,128)} copy(f32[2,64,2048]{2,1,0:T(8,128)S(1)} %get-tuple-element.3) | data formatting | bytes 2097152
